TPU v7x, 128 devices: a whole 4x4x4 slice. The times are simulated.
128 devices in a mesh: row: 16 (over y, z), col: 8 (over x, core).
Axes of the slice: x: 4, y: 4, z: 4, core: 2. Of those that a mesh axis runs over, the one named last changes fastest.
Arguments:
- pair_list: int32 [512, 2], P(('row', 'col')), may hold values from 0 to 127, as said below
- jacobian: float32 [512, 1024, 256], P(('row', 'col'))
- damping: float32 [16384], P('row'), may hold values from 0.5 to 2
Outputs:
- factor: float32 [16384, 1024], P('row')
- trailing: float32 [16384, 16384], P('row', 'col')
Inputs may be any that keep to these rules, and one draw needn't show every extreme that they name: `pair_list`: for pair p with entries (a, b): 0 <= b < a, and a lies in block row p // 32 of 8 subapertures, that is a * 16 // 128 equals it. A pair may appear more than once.
All inputs are finite; a program needn't handle non-finite values.
Results may differ from a plain program's by a relative error of at most 0.0001.
Values sent between devices are 32-bit elements; how exact they have to be, the bound alone decides.
No kernel may reach another device: no remote copies, remote signals or barrier semaphores. Data moves between devices by JAX's collectives and lax.ppermute only.
A program may use at most 128 MiB of HBM per device.

v0:
```python
import jax
import jax.numpy as jnp
from jax import lax
from jax.experimental import pallas as pl
from jax.experimental.pallas import tpu as pltpu
from jax.sharding import PartitionSpec as P

F32 = jnp.float32
BF16 = jnp.bfloat16
HI = lax.Precision.HIGHEST
BOTH = ("row", "col")
NROW, NCOL = 16, 8
NDEV = NROW * NCOL
TILE = 128
LEAD = 8
SLOTS1 = 16
SLOTS2 = 40
DAMP_SLOT = 36
VMEM = pltpu.VMEM
SMEM = pltpu.SMEM


def nt(a, b, precision=None):
    return lax.dot_general(
        a, b, (((1,), (1,)), ((), ())), precision=precision, preferred_element_type=F32
    )


def tn(a, b, precision=None):
    return lax.dot_general(
        a, b, (((0,), (0,)), ((), ())), precision=precision, preferred_element_type=F32
    )


def split(x):
    high = x.astype(BF16)
    return high, (x - high.astype(F32)).astype(BF16)


def nt3(ah, al, bh, bl):
    return nt(ah, bh) + (nt(ah, bl) + nt(al, bh))


def nn3(ah, al, bh, bl):
    def nn(a, b):
        return jnp.dot(a, b, preferred_element_type=F32)

    return nn(ah, bh) + (nn(ah, bl) + nn(al, bh))


def first_tile(b):
    return b * LEAD - (b * (b - 1)) // 2


def gram_kernel(jac_ref, idx_ref, damp_ref, pay_ref, cross_ref):
    q = pl.program_id(0)
    high, low = split(jac_ref[0])
    mixed = tn(high, low)
    gram = tn(high, high) + (mixed + mixed.T)
    pay_ref[pl.ds(q, TILE, stride=SLOTS1), :] = gram[:TILE, :TILE]
    pay_ref[pl.ds(q + 4, TILE, stride=SLOTS1), :] = gram[TILE:, TILE:]
    pay_ref[pl.ds(q + 8, TILE, stride=SLOTS1), :] = gram[:TILE, TILE:]
    cross_ref[0] = gram[:TILE, TILE:]

    @pl.when(q == 0)
    def _():
        lane = lax.broadcasted_iota(jnp.int32, (TILE, TILE), 1)
        index = jnp.zeros((TILE, TILE), F32)
        for e in range(8):
            index = jnp.where(lane == e, idx_ref[e // 2, e % 2].astype(F32), index)
        pay_ref[pl.ds(12, TILE, stride=SLOTS1), :] = index
        rows = [damp_ref[TILE * b : TILE * (b + 1)].reshape(1, TILE) for b in range(LEAD)]
        wide = jnp.concatenate(rows + [jnp.zeros((TILE - 8, TILE), F32)], axis=0)
        pay_ref[pl.ds(13, TILE, stride=SLOTS1), :] = wide.T
        zero = jnp.zeros((TILE, TILE), F32)
        pay_ref[pl.ds(14, TILE, stride=SLOTS1), :] = zero
        pay_ref[pl.ds(15, TILE, stride=SLOTS1), :] = zero


def grams(jacobian, idx, damp):
    return pl.pallas_call(
        gram_kernel,
        grid=(4,),
        in_specs=[
            pl.BlockSpec((1, 1024, 256), lambda q: (q, 0, 0)),
            pl.BlockSpec(memory_space=SMEM),
            pl.BlockSpec((1024,), lambda q: (0,)),
        ],
        out_specs=[
            pl.BlockSpec((TILE * SLOTS1, TILE), lambda q: (0, 0)),
            pl.BlockSpec((1, TILE, TILE), lambda q: (q, 0, 0)),
        ],
        out_shape=[
            jax.ShapeDtypeStruct((TILE * SLOTS1, TILE), F32),
            jax.ShapeDtypeStruct((4, TILE, TILE), F32),
        ],
        name="grams",
    )(jacobian, idx, damp)


def gather_kernel(recv_ref, pay_ref, diag_ref, idx_ref):
    lane = lax.broadcasted_iota(jnp.int32, (TILE, TILE), 1)
    sub = lax.broadcasted_iota(jnp.int32, (TILE, TILE), 0)
    index = recv_ref[pl.ds(12, NDEV, stride=SLOTS1), :].astype(jnp.int32)
    idx_ref[...] = index
    across = recv_ref[pl.ds(12, NDEV, stride=SLOTS1), :].T.astype(jnp.int32)
    diag = jnp.zeros((TILE, TILE), F32)
    lead = jnp.zeros((40, TILE), F32)
    sub40 = lax.broadcasted_iota(jnp.int32, (40, TILE), 0)
    lane40 = lax.broadcasted_iota(jnp.int32, (40, TILE), 1)
    for q in range(4):
        a = across[2 * q : 2 * q + 1, :]
        b = across[2 * q + 1 : 2 * q + 2, :]
        first = recv_ref[pl.ds(q, NDEV, stride=SLOTS1), :]
        second = recv_ref[pl.ds(q + 4, NDEV, stride=SLOTS1), :]
        cross = recv_ref[pl.ds(q + 8, NDEV, stride=SLOTS1), :]
        diag = diag + jnp.dot((sub == a).astype(F32), first, precision=HI)
        diag = diag + jnp.dot((sub == b).astype(F32), second, precision=HI)
        place = first_tile(b) + (a - b)
        hit = (sub40 == place) & (lane40 < NCOL)
        lead = lead + jnp.dot(hit.astype(F32), cross, precision=HI)
    hit = (sub40 == first_tile(lane40)) & (lane40 < LEAD)
    lead = lead + jnp.dot(hit.astype(F32), diag, precision=HI)
    damp = jnp.broadcast_to(recv_ref[13:14, :], (40, TILE))
    lead = jnp.where(sub40 == DAMP_SLOT, damp, lead)
    for r in range(NROW):
        for c in range(NCOL):
            device = r * NCOL + c
            pay_ref[device * SLOTS2 : (device + 1) * SLOTS2, :] = lead
            diag_ref[device * LEAD : (device + 1) * LEAD, :] = diag[8 * r : 8 * r + 8, :]


def gather_rows(recv):
    return pl.pallas_call(
        gather_kernel,
        out_shape=[
            jax.ShapeDtypeStruct((NDEV * SLOTS2, TILE), F32),
            jax.ShapeDtypeStruct((NDEV * LEAD, TILE), F32),
            jax.ShapeDtypeStruct((NDEV, TILE), jnp.int32),
        ],
        name="gather_rows",
    )(recv)


def pieces(x):
    high = x.astype(BF16).astype(F32)
    rest = x - high
    mid = rest.astype(BF16).astype(F32)
    return high, mid, rest - mid


def factor128(rows):
    lane = lax.broadcasted_iota(jnp.int32, (8, TILE), 1)
    sub = lax.broadcasted_iota(jnp.int32, (8, TILE), 0)
    block = list(rows)
    inv = [jnp.where(lane == sub + 8 * v, 1.0, 0.0) for v in range(16)]
    upper, inverse = [], []

    def row(x, i):
        return jnp.broadcast_to(x[i : i + 1, :], (8, TILE))

    def col(x, i):
        return jnp.broadcast_to(x[:, i : i + 1], (8, TILE))

    for t in range(16):
        cols = [col(block[t], 8 * t + k) for k in range(8)]
        left, right = block[t], inv[t]
        up = jnp.zeros((8, TILE), F32)
        low = up
        for j in range(0, 8, 2):
            one, two = sub == j, sub == j + 1
            both = one | two
            x, y = cols[j], cols[j + 1]
            p, b, q = row(x, j), row(x, j + 1), row(y, j + 1)
            det = p * q - b * b
            over = 1.0 / det
            n1 = jnp.where(one, -q, jnp.where(two, b, x * q - y * b))
            n2 = jnp.where(one, b, jnp.where(two, -p, y * p - x * b))
            for k in range(j + 2, 8):
                change = (n1 * row(cols[k], j) + n2 * row(cols[k], j + 1)) * over
                cols[k] = jnp.where(both, 0.0, cols[k]) - change
            m1, m2 = n1 * over, n2 * over
            inv_p = 1.0 / p
            root_1, root_2, ratio = lax.rsqrt(p), lax.rsqrt(det * inv_p), b * inv_p
            l1, l2, r1, r2 = row(left, j), row(left, j + 1), row(right, j), row(right, j + 1)
            up = jnp.where(one, l1 * root_1, jnp.where(two, (l2 - ratio * l1) * root_2, up))
            low = jnp.where(one, r1 * root_1, jnp.where(two, (r2 - ratio * r1) * root_2, low))
            left = jnp.where(both, 0.0, left) - (m1 * l1 + m2 * l2)
            right = jnp.where(both, 0.0, right) - (m1 * r1 + m2 * r2)
        upper.append(jnp.where(lane >= sub + 8 * t, up, 0.0))
        inverse.append(low)
        if t < 15:
            parts = [col(block[t + 1], 8 * t + k) for k in range(8)]
            one = [parts[k] * row(left, k) for k in range(8)]
            two = [parts[k] * row(right, k) for k in range(8)]
            while len(one) > 1:
                one = [one[i] + one[i + 1] for i in range(0, len(one), 2)]
                two = [two[i] + two[i + 1] for i in range(0, len(two), 2)]
            block[t + 1] = block[t + 1] - one[0]
            inv[t + 1] = inv[t + 1] - two[0]
        if t < 14:
            h, m, low_part = pieces(block[t])
            mult = jnp.concatenate([h, h, m, h, low_part, m], axis=0).T.astype(BF16)
            h, m, low_part = pieces(jnp.concatenate([left, right], axis=1))
            base = jnp.concatenate([h, m, h, low_part, h, m], axis=0).astype(BF16)
            late = jnp.dot(mult, base, preferred_element_type=F32)
            for v in range(t + 2, 16):
                block[v] = block[v] - late[8 * v : 8 * v + 8, :TILE]
                inv[v] = inv[v] - late[8 * v : 8 * v + 8, TILE:]
    return upper, inverse


def at(i, n=TILE):
    return pl.ds(pl.multiple_of(i * n, n), n)


def three(x):
    high = x.astype(BF16)
    rest = x - high.astype(F32)
    mid = rest.astype(BF16)
    return high, mid, (rest - mid.astype(F32)).astype(BF16)


def stacks(x):
    h, m, low = three(x)
    return (
        jnp.concatenate([h, h], axis=1),
        jnp.concatenate([m, h], axis=1),
        jnp.concatenate([low, m], axis=1),
    )


def right_stacks(x):
    h, m, low = three(x)
    return jnp.concatenate([h, m], axis=1), jnp.concatenate([h, low], axis=1)


def six(pa, pb, pc, ra, rb):
    return nt(pa, ra) + (nt(pb, rb) + nt(pc, ra))


def nn(a, b):
    return jnp.dot(a, b, precision=HI, preferred_element_type=F32)


def factor_kernel(
    recv_ref, lh_hbm, ll_hbm, wh_hbm, wl_hbm,
    lh_ref, ll_ref, wh_ref, wl_ref, body, inv_ref, pa, pb, pc, ra, rb, sem,
):
    place = 0
    lane = lax.broadcasted_iota(jnp.int32, (TILE, TILE), 1)
    sub = lax.broadcasted_iota(jnp.int32, (TILE, TILE), 0)
    damp = recv_ref[pl.ds(DAMP_SLOT, TILE, stride=SLOTS2), :]
    for k in range(LEAD):
        for i in range(k, LEAD):
            tile = recv_ref[pl.ds(place, TILE, stride=SLOTS2), :]
            if i == k:
                tile = tile + jnp.where(lane == sub, damp[:, k : k + 1], 0.0)
            body[TILE * i : TILE * (i + 1), TILE * k : TILE * (k + 1)] = tile
            place += 1

    def step(k, _):
        rows = [
            body[pl.ds(pl.multiple_of(k * TILE + 8 * v, 8), 8), at(k)] for v in range(16)
        ]
        upper, inverse = factor128(rows)
        inv = jnp.concatenate(inverse, axis=0)
        inv_ref[at(k), :] = inv
        wa, wb = right_stacks(inv)

        def panel(i, _):
            x = six(*stacks(body[at(i, 512), at(k)]), wa, wb)
            index = i * 512 + lax.broadcasted_iota(jnp.int32, (512, TILE), 0)
            x = jnp.where(index >= (k + 1) * TILE, x, 0.0)
            h, m, low = three(x)
            pa[at(i, 512), :] = jnp.concatenate([h, h], axis=1)
            pb[at(i, 512), :] = jnp.concatenate([m, h], axis=1)
            pc[at(i, 512), :] = jnp.concatenate([low, m], axis=1)
            ra[at(i, 512), :] = jnp.concatenate([h, m], axis=1)
            rb[at(i, 512), :] = jnp.concatenate([h, low], axis=1)
            lh_ref[at(i, 512), at(k)] = h
            ll_ref[at(i, 512), at(k)] = m
            return 0

        begin = (k >= 3).astype(jnp.int32)

        @pl.when(k >= 3)
        def _():
            zero = jnp.zeros((512, TILE), BF16)
            lh_ref[:512, at(k)] = zero
            ll_ref[:512, at(k)] = zero

        lax.fori_loop(begin, 2, panel, 0)

        def update(j, _):
            wa, wb = ra[at(j, 256), :], rb[at(j, 256), :]

            def rows_of(i, _):
                part = at(i, 512)
                body[part, at(j, 256)] -= six(pa[part, :], pb[part, :], pc[part, :], wa, wb)
                return 0

            lax.fori_loop((j >= 2).astype(jnp.int32), 2, rows_of, 0)
            return 0

        lax.fori_loop((k + 1) // 2, 4, update, 0)
        tile = jnp.concatenate(upper, axis=0).T
        body[at(k), at(k)] = tile
        lh_ref[at(k), at(k)], ll_ref[at(k), at(k)] = split(tile)
        pltpu.make_async_copy(lh_ref.at[:, at(k)], lh_hbm.at[:, at(k)], sem.at[0]).start()
        pltpu.make_async_copy(ll_ref.at[:, at(k)], ll_hbm.at[:, at(k)], sem.at[1]).start()
        return 0

    lax.fori_loop(0, LEAD, step, 0)
    for g in range(4):
        one = slice(256 * g, 256 * g + TILE)
        two = slice(256 * g + TILE, 256 * g + 256)
        cross = lh_ref[two, one].astype(F32) + ll_ref[two, one].astype(F32)
        corner = -nn(inv_ref[two, :], nn(cross, inv_ref[one, :]))
        wh_ref[one, :TILE], wl_ref[one, :TILE] = split(inv_ref[one, :])
        zero = jnp.zeros((TILE, TILE), BF16)
        wh_ref[one, TILE:], wl_ref[one, TILE:] = zero, zero
        wh_ref[two, :TILE], wl_ref[two, :TILE] = split(corner)
        wh_ref[two, TILE:], wl_ref[two, TILE:] = split(inv_ref[two, :])
    last = [
        pltpu.make_async_copy(wh_ref, wh_hbm, sem.at[2]),
        pltpu.make_async_copy(wl_ref, wl_hbm, sem.at[3]),
    ]
    for copy in last:
        copy.start()
    pltpu.make_async_copy(lh_ref, lh_hbm, sem.at[0]).wait()
    pltpu.make_async_copy(ll_ref, ll_hbm, sem.at[1]).wait()
    for copy in last:
        copy.wait()


def factorise(recv):
    return pl.pallas_call(
        factor_kernel,
        in_specs=[pl.BlockSpec(memory_space=VMEM)],
        out_specs=[pl.BlockSpec(memory_space=pltpu.HBM)] * 4,
        out_shape=[
            jax.ShapeDtypeStruct((1024, 1024), BF16),
            jax.ShapeDtypeStruct((1024, 1024), BF16),
            jax.ShapeDtypeStruct((1024, 256), BF16),
            jax.ShapeDtypeStruct((1024, 256), BF16),
        ],
        scratch_shapes=[VMEM((1024, 1024), BF16)] * 2
        + [VMEM((1024, 256), BF16)] * 2
        + [VMEM((1024, 1024), F32), VMEM((1024, TILE), F32)]
        + [VMEM((1024, 256), BF16)] * 5
        + [pltpu.SemaphoreType.DMA((4,))],
        compiler_params=pltpu.CompilerParams(vmem_limit_bytes=58 * 1024 * 1024),
        cost_estimate=pl.CostEstimate(
            flops=40_000_000_000, bytes_accessed=8_000_000, transcendentals=0
        ),
        name="factorise",
    )(recv)


def schur_kernel(
    scal_ref, damp_ref, lh_hbm, ll_hbm, wh_hbm, wl_hbm, col_hbm, cross_hbm, diag_hbm,
    factor_hbm, out_hbm,
    lh_ref, ll_ref, wh_ref, wl_ref, col_ref, cross_ref, diag_ref, out_ref, rows, cols,
    xh, xl, yh, yl, bh, bl, none_ref, where_ref, row_tiles, col_tiles, used_ref,
    load_sem, factor_sem, out_sem,
):
    row = scal_ref[192]
    column = scal_ref[193]
    loads = [
        pltpu.make_async_copy(source, target, load_sem.at[i])
        for i, (source, target) in enumerate(
            [
                (cross_hbm, cross_ref),
                (col_hbm, col_ref),
                (diag_hbm, diag_ref),
                (lh_hbm, lh_ref),
                (ll_hbm, ll_ref),
                (wh_hbm, wh_ref),
                (wl_hbm, wl_ref),
            ]
        )
    ]
    for copy in loads:
        copy.start()
    none_ref[...] = jnp.zeros_like(none_ref)
    for u in range(24):
        where_ref[u] = 0
    for u in range(64):
        used_ref[u] = 0

    def mark_row(p, _):
        a = scal_ref[2 * p] - LEAD * row
        where_ref[a] = jnp.where(scal_ref[2 * p + 1] < LEAD, 1, where_ref[a])
        return 0

    def mark_col(p, _):
        tile = scal_ref[64 + 2 * p]
        a = tile - 16 * column + LEAD
        b = scal_ref[65 + 2 * p]

        @pl.when((b < LEAD) & (tile >= LEAD) & (tile <= LEAD * row + 7))
        def _():
            where_ref[a] = 1
            used_ref[4 * (a - LEAD) + b // 2] = 1

        return 0

    @pl.when(row >= 1)
    def _():
        lax.fori_loop(0, 32, mark_row, 0)
        lax.fori_loop(0, 64, mark_col, 0)

    def place_row(u, count):
        used = where_ref[u] == 1
        where_ref[u] = jnp.where(used, count, -1)
        row_tiles[count] = u
        return count + used.astype(jnp.int32)

    def place_col(u, count):
        used = where_ref[u + LEAD] == 1
        where_ref[u + LEAD] = jnp.where(used, count, -1)
        col_tiles[count] = u
        return count + used.astype(jnp.int32)

    n_row = lax.fori_loop(0, LEAD, place_row, jnp.int32(0))
    n_col = lax.fori_loop(0, 16, place_col, jnp.int32(0))

    def blank(i, _):
        out_ref[at(i, 32), :] = jnp.zeros((32, 2048), F32)
        return 0

    lax.fori_loop(0, 32, blank, 0)

    def clear(i, _):
        rows[at(i), :] = jnp.zeros((TILE, 1024), F32)
        return 0

    lax.fori_loop(0, n_row, clear, 0)

    def clear_cols(i, _):
        cols[at(i), :] = jnp.zeros((TILE, 1024), F32)
        return 0

    lax.fori_loop(0, n_col, clear_cols, 0)
    loads[0].wait()

    def fill_row(p, _):
        a = scal_ref[2 * p] - LEAD * row
        b = scal_ref[2 * p + 1]
        here = b - 16 * column

        @pl.when((b < LEAD) & (where_ref[a] >= 0))
        def _():
            rows[at(where_ref[a]), at(b)] += cross_ref[at(p), :]

        @pl.when((b >= LEAD) & (here >= 0) & (here < 16))
        def _():
            out_ref[at(a), at(here)] += cross_ref[at(p), :]

        return 0

    def fill_col(p, _):
        a = scal_ref[64 + 2 * p] - 16 * column + LEAD
        b = scal_ref[65 + 2 * p]

        @pl.when((b < LEAD) & (where_ref[a] >= 0))
        def _():
            cols[at(where_ref[a]), at(b)] += col_ref[at(p), :]

        return 0

    lax.fori_loop(0, 32, fill_row, 0)
    loads[1].wait()
    lax.fori_loop(0, 64, fill_col, 0)
    loads[2].wait()

    @pl.when((row >= 1) & (row // 2 == column))
    def _():
        lane = lax.broadcasted_iota(jnp.int32, (TILE, TILE), 1)
        sub = lax.broadcasted_iota(jnp.int32, (TILE, TILE), 0)
        for s in range(LEAD):
            damp = damp_ref[TILE * s : TILE * (s + 1)].reshape(1, TILE)
            damp = jnp.broadcast_to(damp, (TILE, TILE))
            tile = diag_ref[pl.ds(s, TILE, stride=LEAD), :] + jnp.where(lane == sub, damp, 0.0)
            out_ref[TILE * s : TILE * (s + 1), at(LEAD * (row % 2) + s)] += tile

    for copy in loads[3:]:
        copy.wait()

    chunks = (n_row + 1) // 2
    for g in range(4):
        here = slice(256 * g, 256 * (g + 1))

        def forward(i, _, g=g, here=here):
            part = at(i, 256)
            rest = rows[part, here]
            if g:
                rest = rest - nt3(
                    xh[part, : 256 * g],
                    xl[part, : 256 * g],
                    lh_ref[here, : 256 * g],
                    ll_ref[here, : 256 * g],
                )
            x = nt3(*split(rest), wh_ref[here, :], wl_ref[here, :])
            rows[part, here] = x
            xh[part, here], xl[part, here] = split(x)
            return 0

        lax.fori_loop(0, chunks, forward, 0)

    for s in range(LEAD):
        part = slice(TILE * s, TILE * (s + 1))

        @pl.when(row == 0)
        def _(part=part):
            rows[part, :] = lh_ref[part, :].astype(F32) + ll_ref[part, :].astype(F32)
            pltpu.make_async_copy(rows.at[part], factor_hbm.at[part], factor_sem.at[0]).start()

        @pl.when((row >= 1) & (where_ref[s] >= 0))
        def _(s=s, part=part):
            pltpu.make_async_copy(
                rows.at[at(where_ref[s])], factor_hbm.at[part], factor_sem.at[0]
            ).start()

        @pl.when((row >= 1) & (where_ref[s] < 0))
        def _(part=part):
            pltpu.make_async_copy(none_ref, factor_hbm.at[part], factor_sem.at[0]).start()

    for g in reversed(range(4)):
        here = slice(256 * g, 256 * (g + 1))

        def backward(i, _, g=g, here=here):
            part = at(i, 256)
            rest = rows[part, here]
            if g < 3:
                past = slice(256 * (g + 1), 1024)
                rest = rest - nn3(
                    yh[part, past], yl[part, past], lh_ref[past, here], ll_ref[past, here]
                )
            yh[part, here], yl[part, here] = split(
                nn3(*split(rest), wh_ref[here, :], wl_ref[here, :])
            )
            return 0

        lax.fori_loop(0, chunks, backward, 0)

    def send(c):
        part = at(c)
        pltpu.make_async_copy(out_ref.at[:, part], out_hbm.at[:, part], out_sem.at[0]).start()

    def columns(j, sent):
        one_tile = col_tiles[2 * j]
        two_tile = col_tiles[jnp.minimum(2 * j + 1, n_col - 1)]

        def chunk(c, _):
            @pl.when((used_ref[4 * one_tile + c] | used_ref[4 * two_tile + c]) == 1)
            def _():
                bh[...], bl[...] = split(cols[at(j, 256), at(c, 256)])

                def blocks(i, _):
                    left = (at(i, 256), at(c, 256))
                    prod = nt3(yh[left], yl[left], bh[...], bl[...])
                    for p in range(2):
                        for q in range(2):
                            it = 2 * i + p
                            a = row_tiles[it]
                            b = two_tile if q else one_tile
                            keep = (it < n_row) & (LEAD * row + a >= 16 * column + b)
                            if q:
                                keep = keep & (2 * j + 1 < n_col)

                            @pl.when(keep)
                            def _(a=a, b=b, p=p, q=q):
                                out_ref[at(a), at(b)] -= prod[
                                    TILE * p : TILE * (p + 1), TILE * q : TILE * (q + 1)
                                ]

                    return 0

                lax.fori_loop(0, chunks, blocks, 0)

            return 0

        lax.fori_loop(0, 4, chunk, 0)
        done = two_tile + 1

        def one(c, _):
            send(c)
            return 0

        lax.fori_loop(sent, done, one, 0)
        return done

    sent = lax.fori_loop(0, (n_col + 1) // 2, columns, jnp.int32(0))

    def last(c, _):
        send(c)
        return 0

    lax.fori_loop(sent, 16, last, 0)
    pltpu.make_async_copy(rows, factor_hbm, factor_sem.at[0]).wait()
    pltpu.make_async_copy(out_ref, out_hbm, out_sem.at[0]).wait()


def schur(scal, lh, ll, wh, wl, col_cross, cross, diag, damp):
    return pl.pallas_call(
        schur_kernel,
        in_specs=[pl.BlockSpec(memory_space=SMEM), pl.BlockSpec(memory_space=VMEM)]
        + [pl.BlockSpec(memory_space=pltpu.HBM)] * 7,
        out_specs=[pl.BlockSpec(memory_space=pl.ANY)] * 2,
        out_shape=[
            jax.ShapeDtypeStruct((1024, 1024), F32),
            jax.ShapeDtypeStruct((1024, 2048), F32),
        ],
        scratch_shapes=[
            VMEM((1024, 1024), BF16),
            VMEM((1024, 1024), BF16),
            VMEM((1024, 256), BF16),
            VMEM((1024, 256), BF16),
            VMEM((64 * TILE, TILE), F32),
            VMEM((32 * TILE, TILE), F32),
            VMEM((NDEV * LEAD, TILE), F32),
            VMEM((1024, 2048), F32),
            VMEM((1024, 1024), F32),
            VMEM((2048, 1024), F32),
            VMEM((1024, 1024), BF16),
            VMEM((1024, 1024), BF16),
            VMEM((1024, 1024), BF16),
            VMEM((1024, 1024), BF16),
            VMEM((256, 256), BF16),
            VMEM((256, 256), BF16),
            VMEM((TILE, 1024), F32),
            SMEM((24,), jnp.int32),
            SMEM((9,), jnp.int32),
            SMEM((17,), jnp.int32),
            SMEM((64,), jnp.int32),
            pltpu.SemaphoreType.DMA((7,)),
            pltpu.SemaphoreType.DMA((1,)),
            pltpu.SemaphoreType.DMA((1,)),
        ],
        compiler_params=pltpu.CompilerParams(vmem_limit_bytes=60 * 1024 * 1024),
        cost_estimate=pl.CostEstimate(
            flops=20_000_000_000, bytes_accessed=30_000_000, transcendentals=0
        ),
        name="schur",
    )(scal, damp, lh, ll, wh, wl, col_cross, cross, diag)


def local(pair_list, jacobian, damping):
    row = lax.axis_index("row")
    column = lax.axis_index("col")
    payload, cross = grams(jacobian, pair_list, damping)
    recv = lax.all_to_all(payload.reshape(NDEV, SLOTS1, TILE), BOTH, 0, 0, tiled=True)
    cross = cross.reshape(4 * TILE, TILE)
    moves = [
        (r * NCOL + c, (NCOL * (r % 2) + c) * NCOL + r // 2) for r in range(NROW) for c in range(NCOL)
    ]
    moved = lax.ppermute(cross, BOTH, moves)
    row_cross = lax.all_gather(cross, "col", axis=0, tiled=True)
    payload, diag, index = gather_rows(recv.reshape(NDEV * SLOTS1, TILE))
    recv = lax.all_to_all(payload.reshape(NDEV, SLOTS2, TILE), BOTH, 0, 0, tiled=True)
    recv, diag, moved = lax.optimization_barrier((recv, diag, moved))
    col_cross = lax.all_gather(moved, "row", axis=0, tiled=True)
    diag = lax.all_to_all(diag.reshape(NDEV, LEAD, TILE), BOTH, 0, 0, tiled=True)
    diag = diag.reshape(NDEV * LEAD, TILE)
    lh, ll, wh, wl = factorise(recv.reshape(NDEV * SLOTS2, TILE))

    index = index[:, :8].reshape(NDEV * 8)
    scal = jnp.concatenate(
        [
            lax.dynamic_slice(index, (row * 64,), (64,)),
            lax.dynamic_slice(index, (column * 128,), (128,)),
            jnp.stack([row, column]).astype(jnp.int32),
        ]
    )
    return tuple(schur(scal, lh, ll, wh, wl, col_cross, row_cross, diag, damping))


def solution(mesh):
    placed = (P(("row", "col"), None), P(("row", "col"), None, None), P("row"))
    return jax.shard_map(
        local,
        mesh=mesh,
        in_specs=placed,
        out_specs=(P("row", None), P("row", "col")),
        check_vma=False,
    )
```

profile of v0, /device:TPU:32, one launch (start us, length us, event | category | flops | bytes accessed | tf_op | source)
XLA Modules:
  0.0 211.4 jit_solution(5445915245050870382)
XLA Ops:
  7.2 0.0 all-gather.5.cloned.1.call-start
  7.2 1.3 copy.6.idx_ref
  8.5 5.5 %grams.1 = (f32[2048,128]{1,0:T(8,128)}, f32[4,128,128]{2,1,0:T(8,128)}) custom-call(f32[4,1024,256]{2,1,0:T(8,128)} %jac_ref.1, s32[4,2]{1,0:T(4,128)} %copy.6.idx_ref, f32[1024]{0:T(1024)} %damp_ref.3), custom_call_target="tpu_custom_call" | custom-call | tf_op jit(solution)/shard_map/grams/pallas_call | solution.py:81
  14.0 0.0 all-gather.5.cloned.1.call-update
  14.0 34.7 %all_to_all.15 = f32[128,16,128]{2,1,0:T(8,128)} all-to-all(f32[128,16,128]{2,1,0:T(8,128)} %bitcast.13), channel_id=1, replica_groups=mesh['row'=16,'col'=8] {'row','col'}, dimensions={0} | all-to-all | bytes 2097152 | tf_op jit(solution)/shard_map/all_to_all | solution.py:654
  48.7 4.1 %gather_rows.1 = (f32[5120,128]{1,0:T(8,128)}, f32[1024,128]{1,0:T(8,128)}, s32[128,128]{1,0:T(8,128)}) custom-call(f32[2048,128]{1,0:T(8,128)} %bitcast.10), custom_call_target="tpu_custom_call" | custom-call | tf_op jit(solution)/shard_map/gather_rows/pallas_call | solution.py:134
  52.8 0.0 copy-start.2
  52.8 0.0 copy-start.4
  52.8 8.0 %all-to-all-start.1 = ((f32[128,40,128]{2,1,0:T(8,128)}), f32[128,40,128]{2,1,0:T(8,128)S(1)}, u32[]{:S(2)}, u32[]{:S(2)}) async-start(f32[128,40,128]{2,1,0:T(8,128)} %bitcast.12), calls=%async_computation.1 | async-start | bytes 5242880 | tf_op jit(solution)/shard_map/all_to_all | solution.py:662
  60.8 0.0 all-gather.3.cloned.1.call-start
  60.8 0.0 copy-done.2
  60.9 4.7 %collective-permute-start = (f32[512,128]{1,0:T(8,128)S(1)}, f32[512,128]{1,0:T(8,128)S(1)}, u32[]{:S(2)}, u32[]{:S(2)}) collective-permute-start(f32[512,128]{1,0:T(8,128)S(1)} %bitcast.16), channel_id=1, source_target_pairs={{0,0},{1,8},{2,16},{3,24},{4,32},{5,40},{6,48},{7,56},{8,64},{9,72... | collective-permute-start | bytes 786440 | tf_op jit(solution)/shard_map/ppermute | solution.py:659
  65.6 34.5 %collective-permute-done = f32[512,128]{1,0:T(8,128)S(1)} collective-permute-done((f32[512,128]{1,0:T(8,128)S(1)}, f32[512,128]{1,0:T(8,128)S(1)}, u32[]{:S(2)}, u32[]{:S(2)}) %collective-permute-start) | collective-permute-done | bytes 262176 | tf_op jit(solution)/shard_map/ppermute | solution.py:659
  100.1 0.0 copy-start.3
  100.1 0.0 all-to-all-done.1
  100.1 0.0 copy-start
  100.1 0.7 copy-done.3
  100.8 0.0 all-gather.3.cloned.1.call-update
  100.8 0.0 copy-done.4
  100.9 0.1 reshape.30
  101.0 0.1 dynamic_slice.7
  101.0 0.1 dynamic_slice.6
  101.1 0.7 pad_add_fusion.scal_ref
  101.8 10.9 %all-to-all-start.2 = ((f32[128,8,128]{2,1,0:T(8,128)}), f32[128,8,128]{2,1,0:T(8,128)S(1)}, u32[]{:S(2)}, u32[]{:S(2)}) async-start(f32[128,8,128]{2,1,0:T(8,128)} %bitcast.7), calls=%async_computation.2 | async-start | bytes 1048576 | tf_op jit(solution)/shard_map/all_to_all | solution.py:665
  112.7 0.0 copy-done
  112.7 44.7 %factorise.1 = (bf16[1024,1024]{1,0:T(8,128)(2,1)}, bf16[1024,1024]{1,0:T(8,128)(2,1)}, bf16[1024,256]{1,0:T(8,128)(2,1)}, bf16[1024,256]{1,0:T(8,128)(2,1)}) custom-call(f32[5120,128]{1,0:T(8,128)} %bitcast.11), custom_call_target="tpu_custom_call" | custom-call | flops 40000000000 | bytes 8000000 | tf_op jit(solution)/shard_map/factorise/pallas_call | solution.py:338
  157.4 0.0 all-gather.5.cloned.1.call-done.cross_hbm
  157.4 0.0 all-to-all-done.2
  157.5 0.0 copy-start.1
  157.5 1.7 all-gather.3.cloned.1.call-done.col_hbm
  159.2 0.0 copy-done.1
  159.2 45.3 %schur.1 = (f32[1024,1024]{1,0:T(8,128)}, f32[1024,2048]{1,0:T(8,128)}) custom-call(s32[194]{0:T(256)} %pad_add_fusion.scal_ref, f32[1024]{0:T(1024)} %damp_ref.3, bf16[1024,1024]{1,0:T(8,128)(2,1)} %get-tuple-element.20.lh_hbm, bf16[1024,1024]{1,0:T(8,128)(2,1)} %get-tuple-element.21.ll_hbm, bf16[1024,256]{1,0:T(8,128)(2,1)} %get-tuple-element.22.wh_hbm, ...), custom_call_target="tpu_custom_call" | custom-call | flops 20000000000 | bytes 30000000 | tf_op jit(solution)/shard_map/schur/pallas_call | solution.py:607
Async XLA Ops:
  7.2 150.3 %all-gather.5.cloned.1.call-start = ((), (), s32[]{:S(2)}) async-start(), calls=%async_computation.4 | async-start | bytes 2359296 | tf_op jit(solution)/shard_map/all_gather | solution.py:660
  52.8 8.1 %copy-start.2 = (f32[4,128,128]{2,1,0:T(8,128)S(1)}, f32[4,128,128]{2,1,0:T(8,128)}, u32[]{:S(2)}) copy-start(f32[4,128,128]{2,1,0:T(8,128)} %get-tuple-element.18) | copy-start | bytes 786436
  52.8 48.1 %copy-start.4 = (s32[128,128]{1,0:T(8,128)S(1)}, s32[128,128]{1,0:T(8,128)}, u32[]{:S(2)}) copy-start(s32[128,128]{1,0:T(8,128)} %get-tuple-element.15) | copy-start | bytes 196612
  52.8 47.3 %all-to-all-start.1 = ((f32[128,40,128]{2,1,0:T(8,128)}), f32[128,40,128]{2,1,0:T(8,128)S(1)}, u32[]{:S(2)}, u32[]{:S(2)}) async-start(f32[128,40,128]{2,1,0:T(8,128)} %bitcast.12), calls=%async_computation.1 | async-start | bytes 5242880 | tf_op jit(solution)/shard_map/all_to_all | solution.py:662
  60.8 98.4 %all-gather.3.cloned.1.call-start = ((), (), s32[]{:S(2)}) async-start(), calls=%async_computation.3 | async-start | bytes 4456448 | tf_op jit(solution)/shard_map/all_gather | solution.py:664
  60.9 39.3 %collective-permute-start = (f32[512,128]{1,0:T(8,128)S(1)}, f32[512,128]{1,0:T(8,128)S(1)}, u32[]{:S(2)}, u32[]{:S(2)}) collective-permute-start(f32[512,128]{1,0:T(8,128)S(1)} %bitcast.16), channel_id=1, source_target_pairs={{0,0},{1,8},{2,16},{3,24},{4,32},{5,40},{6,48},{7,56},{8,64},{9,72... | collective-permute-start | bytes 786440 | tf_op jit(solution)/shard_map/ppermute | solution.py:659
  100.1 0.7 copy-start.3
  100.1 12.6 %copy-start = (f32[128,40,128]{2,1,0:T(8,128)}, f32[128,40,128]{2,1,0:T(8,128)S(1)}, u32[]{:S(2)}) copy-start(f32[128,40,128]{2,1,0:T(8,128)S(1)} %all-to-all-done.1) | copy-start | bytes 7864324
  101.8 55.7 %all-to-all-start.2 = ((f32[128,8,128]{2,1,0:T(8,128)}), f32[128,8,128]{2,1,0:T(8,128)S(1)}, u32[]{:S(2)}, u32[]{:S(2)}) async-start(f32[128,8,128]{2,1,0:T(8,128)} %bitcast.7), calls=%async_computation.2 | async-start | bytes 1048576 | tf_op jit(solution)/shard_map/all_to_all | solution.py:665
  157.5 1.8 copy-start.1
Sparse Core Ops, SparseCore 0:
  14.2 34.2 all-gather.4
  101.0 58.2 all-gather.2
where the time goes:
time: 212 us; the launch traced here: 211 us
  Pallas kernels  99.6 us (47%)
  waiting for transfers between devices  36.3 us (17%)
  blocking collectives  34.7 us (16%)
  starting transfers between devices  23.7 us (11%)
  between operations  14.1 us (7%)
  local copies, waits for them, and re-layouts  2.28 us (1%)
    pallas_call x1, Pallas kernels, schur(): pl.pallas_call(schur_kernel, in_specs=[pl.BlockSpec(memory_space=SMEM), p...  45.3 us
    pallas_call x1, Pallas kernels, factorise(): pl.pallas_call(factor_kernel, in_specs=[pl.BlockSpec(memory_space=VMEM)],...  44.7 us
    all_to_all x1, blocking collectives, local(): lax.all_to_all(payload.reshape(NDEV, SLOTS1, TILE), BOTH, 0, 0, tiled=True)  34.7 us
    ppermute x1, waiting for transfers between devices, local(): moved = lax.ppermute(cross, BOTH, moves)  34.5 us
    all_to_all x1, starting transfers between devices, local(): lax.all_to_all(diag.reshape(NDEV, LEAD, TILE), BOTH, 0, 0, tiled=True)  10.9 us
    all_to_all x1, starting transfers between devices, local(): lax.all_to_all(payload.reshape(NDEV, SLOTS2, TILE), BOTH, 0, 0, tiled=True)  8 us
    pallas_call x1, Pallas kernels, grams(): pl.pallas_call(gram_kernel, grid=(4,), in_specs=[pl.BlockSpec((1, 1024, 2...  5.47 us
    ppermute x1, starting transfers between devices, local(): moved = lax.ppermute(cross, BOTH, moves)  4.74 us
  transfers between devices with their start and end apart: 5, of which 2 were waited for; matrix products, arithmetic and copies ran while one was open for 0% of the time, Pallas kernels for 23%

commit v1 on v0

--- a/solution.py
+++ b/solution.py
@@ -15,7 +15,10 @@
 LEAD = 8
 SLOTS1 = 16
 SLOTS2 = 40
-DAMP_SLOT = 36
+PAIR_SLOT = 28
+DAMP_SLOT = 32
+DIAG_SLOT = 33
+OWN_SLOT = 36
 VMEM = pltpu.VMEM
 SMEM = pltpu.SMEM
 
@@ -48,8 +51,8 @@
     return nn(ah, bh) + (nn(ah, bl) + nn(al, bh))
 
 
-def first_tile(b):
-    return b * LEAD - (b * (b - 1)) // 2
+def below_tile(a, b):
+    return b * (LEAD - 1) - (b * (b - 1)) // 2 + (a - b - 1)
 
 
 def gram_kernel(jac_ref, idx_ref, damp_ref, pay_ref, cross_ref):
@@ -67,7 +70,7 @@
         lane = lax.broadcasted_iota(jnp.int32, (TILE, TILE), 1)
         index = jnp.zeros((TILE, TILE), F32)
         for e in range(8):
-            index = jnp.where(lane == e, idx_ref[e // 2, e % 2].astype(F32), index)
+            index = jnp.where(lane == e, idx_ref[e % 2, e // 2].astype(F32), index)
         pay_ref[pl.ds(12, TILE, stride=SLOTS1), :] = index
         rows = [damp_ref[TILE * b : TILE * (b + 1)].reshape(1, TILE) for b in range(LEAD)]
         wide = jnp.concatenate(rows + [jnp.zeros((TILE - 8, TILE), F32)], axis=0)
@@ -98,16 +101,17 @@
     )(jacobian, idx, damp)
 
 
-def gather_kernel(recv_ref, pay_ref, diag_ref, idx_ref):
+def gather_kernel(me_ref, recv_ref, pay_ref, idx_ref, flip_ref):
+    me = me_ref[0]
     lane = lax.broadcasted_iota(jnp.int32, (TILE, TILE), 1)
     sub = lax.broadcasted_iota(jnp.int32, (TILE, TILE), 0)
-    index = recv_ref[pl.ds(12, NDEV, stride=SLOTS1), :].astype(jnp.int32)
-    idx_ref[...] = index
-    across = recv_ref[pl.ds(12, NDEV, stride=SLOTS1), :].T.astype(jnp.int32)
+    index = recv_ref[pl.ds(12, NDEV, stride=SLOTS1), :]
+    idx_ref[...] = index.astype(jnp.int32)
+    across = index.T.astype(jnp.int32)
     diag = jnp.zeros((TILE, TILE), F32)
-    lead = jnp.zeros((40, TILE), F32)
-    sub40 = lax.broadcasted_iota(jnp.int32, (40, TILE), 0)
-    lane40 = lax.broadcasted_iota(jnp.int32, (40, TILE), 1)
+    lead = jnp.zeros((32, TILE), F32)
+    sub32 = lax.broadcasted_iota(jnp.int32, (32, TILE), 0)
+    lane32 = lax.broadcasted_iota(jnp.int32, (32, TILE), 1)
     for q in range(4):
         a = across[2 * q : 2 * q + 1, :]
         b = across[2 * q + 1 : 2 * q + 2, :]
@@ -116,30 +120,36 @@
         cross = recv_ref[pl.ds(q + 8, NDEV, stride=SLOTS1), :]
         diag = diag + jnp.dot((sub == a).astype(F32), first, precision=HI)
         diag = diag + jnp.dot((sub == b).astype(F32), second, precision=HI)
-        place = first_tile(b) + (a - b)
-        hit = (sub40 == place) & (lane40 < NCOL)
+        hit = (sub32 == below_tile(a, b)) & (lane32 < NCOL)
         lead = lead + jnp.dot(hit.astype(F32), cross, precision=HI)
-    hit = (sub40 == first_tile(lane40)) & (lane40 < LEAD)
-    lead = lead + jnp.dot(hit.astype(F32), diag, precision=HI)
-    damp = jnp.broadcast_to(recv_ref[13:14, :], (40, TILE))
-    lead = jnp.where(sub40 == DAMP_SLOT, damp, lead)
+    packed = jnp.where(lane <= me, pltpu.roll(diag, 4, 0), diag)
+    flip_ref[...] = diag.T
+    entries = jnp.broadcast_to(flip_ref[pl.ds(me, 1), :], (8, TILE))
+    damp = jnp.broadcast_to(recv_ref[13:14, :], (8, TILE))
+    sub8 = lax.broadcasted_iota(jnp.int32, (8, TILE), 0)
+    head = jnp.where(sub8 == 0, damp, jnp.where(sub8 == 1, entries, 0.0))
+    last = jnp.where(sub8 >= 4, packed[:8, :], lead[24:, :])
     for r in range(NROW):
+        tail = jnp.where(sub8 >= 4, packed[8 * r : 8 * r + 8, :], head)
         for c in range(NCOL):
-            device = r * NCOL + c
-            pay_ref[device * SLOTS2 : (device + 1) * SLOTS2, :] = lead
-            diag_ref[device * LEAD : (device + 1) * LEAD, :] = diag[8 * r : 8 * r + 8, :]
-
-
-def gather_rows(recv):
+            base = (r * NCOL + c) * SLOTS2
+            pay_ref[base : base + 24, :] = lead[:24, :]
+            pay_ref[base + 24 : base + 32, :] = last
+            pay_ref[base + 32 : base + 40, :] = tail
+
+
+def gather_rows(me, recv):
     return pl.pallas_call(
         gather_kernel,
+        in_specs=[pl.BlockSpec(memory_space=SMEM), pl.BlockSpec(memory_space=VMEM)],
         out_shape=[
             jax.ShapeDtypeStruct((NDEV * SLOTS2, TILE), F32),
-            jax.ShapeDtypeStruct((NDEV * LEAD, TILE), F32),
             jax.ShapeDtypeStruct((NDEV, TILE), jnp.int32),
         ],
+        scratch_shapes=[VMEM((TILE, TILE), F32)],
+        compiler_params=pltpu.CompilerParams(vmem_limit_bytes=16 * 1024 * 1024),
         name="gather_rows",
-    )(recv)
+    )(me, recv)
 
 
 def pieces(x):
@@ -239,6 +249,15 @@
     return nt(pa, ra) + (nt(pb, rb) + nt(pc, ra))
 
 
+def unpack(pair, entries):
+    lane = lax.broadcasted_iota(jnp.int32, (TILE, TILE), 1)
+    sub = lax.broadcasted_iota(jnp.int32, (TILE, TILE), 0)
+    low = jnp.where(lane < sub, pair, 0.0)
+    high = jnp.where(lane > sub, pair, 0.0)
+    one = low + low.T + jnp.where(lane == sub, pair, 0.0)
+    return one, high + high.T + jnp.where(lane == sub, entries, 0.0)
+
+
 def nn(a, b):
     return jnp.dot(a, b, precision=HI, preferred_element_type=F32)
 
@@ -247,17 +266,23 @@
     recv_ref, lh_hbm, ll_hbm, wh_hbm, wl_hbm,
     lh_ref, ll_ref, wh_ref, wl_ref, body, inv_ref, pa, pb, pc, ra, rb, sem,
 ):
-    place = 0
     lane = lax.broadcasted_iota(jnp.int32, (TILE, TILE), 1)
     sub = lax.broadcasted_iota(jnp.int32, (TILE, TILE), 0)
-    damp = recv_ref[pl.ds(DAMP_SLOT, TILE, stride=SLOTS2), :]
+
+    def slot(i):
+        return recv_ref[pl.ds(i, TILE, stride=SLOTS2), :]
+
+    place = 0
     for k in range(LEAD):
-        for i in range(k, LEAD):
-            tile = recv_ref[pl.ds(place, TILE, stride=SLOTS2), :]
-            if i == k:
-                tile = tile + jnp.where(lane == sub, damp[:, k : k + 1], 0.0)
-            body[TILE * i : TILE * (i + 1), TILE * k : TILE * (k + 1)] = tile
+        for i in range(k + 1, LEAD):
+            body[TILE * i : TILE * (i + 1), TILE * k : TILE * (k + 1)] = slot(place)
             place += 1
+    damp, entries = slot(DAMP_SLOT), slot(DIAG_SLOT)
+    for u in range(4):
+        one, two = unpack(slot(PAIR_SLOT + u), entries[:, 4 + u : 5 + u])
+        for k, tile in ((u, one), (u + 4, two)):
+            here = slice(TILE * k, TILE * (k + 1))
+            body[here, here] = tile + jnp.where(lane == sub, damp[:, k : k + 1], 0.0)
 
     def step(k, _):
         rows = [
@@ -359,7 +384,7 @@
 
 
 def schur_kernel(
-    scal_ref, damp_ref, lh_hbm, ll_hbm, wh_hbm, wl_hbm, col_hbm, cross_hbm, diag_hbm,
+    scal_ref, damp_ref, lh_hbm, ll_hbm, wh_hbm, wl_hbm, col_hbm, cross_hbm, recv_hbm,
     factor_hbm, out_hbm,
     lh_ref, ll_ref, wh_ref, wl_ref, col_ref, cross_ref, diag_ref, out_ref, rows, cols,
     xh, xl, yh, yl, bh, bl, none_ref, where_ref, row_tiles, col_tiles, used_ref,
@@ -373,7 +398,7 @@
             [
                 (cross_hbm, cross_ref),
                 (col_hbm, col_ref),
-                (diag_hbm, diag_ref),
+                (recv_hbm.at[:, DAMP_SLOT:SLOTS2], diag_ref),
                 (lh_hbm, lh_ref),
                 (ll_hbm, ll_ref),
                 (wh_hbm, wh_ref),
@@ -479,11 +504,15 @@
     def _():
         lane = lax.broadcasted_iota(jnp.int32, (TILE, TILE), 1)
         sub = lax.broadcasted_iota(jnp.int32, (TILE, TILE), 0)
-        for s in range(LEAD):
-            damp = damp_ref[TILE * s : TILE * (s + 1)].reshape(1, TILE)
-            damp = jnp.broadcast_to(damp, (TILE, TILE))
-            tile = diag_ref[pl.ds(s, TILE, stride=LEAD), :] + jnp.where(lane == sub, damp, 0.0)
-            out_ref[TILE * s : TILE * (s + 1), at(LEAD * (row % 2) + s)] += tile
+        entries = diag_ref[:, DIAG_SLOT - DAMP_SLOT, :]
+        for u in range(4):
+            mine = jnp.where(lane == LEAD * row + 4 + u, entries, 0.0)
+            pair = diag_ref[:, OWN_SLOT - DAMP_SLOT + u, :]
+            one, two = unpack(pair, jnp.sum(mine, axis=1, keepdims=True))
+            for s, tile in ((u, one), (u + 4, two)):
+                damp = damp_ref[TILE * s : TILE * (s + 1)].reshape(1, TILE)
+                damp = jnp.where(lane == sub, jnp.broadcast_to(damp, (TILE, TILE)), 0.0)
+                out_ref[TILE * s : TILE * (s + 1), at(LEAD * (row % 2) + s)] += tile + damp
 
     for copy in loads[3:]:
         copy.wait()
@@ -553,29 +582,50 @@
         one_tile = col_tiles[2 * j]
         two_tile = col_tiles[jnp.minimum(2 * j + 1, n_col - 1)]
 
+        def apply(i, prod):
+            for p in range(2):
+                for q in range(2):
+                    it = 2 * i + p
+                    a = row_tiles[it]
+                    b = two_tile if q else one_tile
+                    keep = (it < n_row) & (LEAD * row + a >= 16 * column + b)
+                    if q:
+                        keep = keep & (2 * j + 1 < n_col)
+
+                    @pl.when(keep)
+                    def _(a=a, b=b, p=p, q=q):
+                        out_ref[at(a), at(b)] -= prod[
+                            TILE * p : TILE * (p + 1), TILE * q : TILE * (q + 1)
+                        ]
+
+        def used(c):
+            return used_ref[4 * one_tile + c] | used_ref[4 * two_tile + c]
+
+        filled = used(0) + used(1) + used(2) + used(3)
+
+        @pl.when(filled > 1)
+        def _():
+            def prepare(c, _):
+                bh[:, at(c, 256)], bl[:, at(c, 256)] = split(cols[at(j, 256), at(c, 256)])
+                return 0
+
+            lax.fori_loop(0, 4, prepare, 0)
+
+            def blocks(i, _):
+                left = at(i, 256)
+                apply(i, nt3(yh[left, :], yl[left, :], bh[...], bl[...]))
+                return 0
+
+            lax.fori_loop(0, chunks, blocks, 0)
+
         def chunk(c, _):
-            @pl.when((used_ref[4 * one_tile + c] | used_ref[4 * two_tile + c]) == 1)
+            @pl.when((filled == 1) & (used(c) == 1))
             def _():
-                bh[...], bl[...] = split(cols[at(j, 256), at(c, 256)])
+                bh[:, :256], bl[:, :256] = split(cols[at(j, 256), at(c, 256)])
 
                 def blocks(i, _):
                     left = (at(i, 256), at(c, 256))
-                    prod = nt3(yh[left], yl[left], bh[...], bl[...])
-                    for p in range(2):
-                        for q in range(2):
-                            it = 2 * i + p
-                            a = row_tiles[it]
-                            b = two_tile if q else one_tile
-                            keep = (it < n_row) & (LEAD * row + a >= 16 * column + b)
-                            if q:
-                                keep = keep & (2 * j + 1 < n_col)
-
-                            @pl.when(keep)
-                            def _(a=a, b=b, p=p, q=q):
-                                out_ref[at(a), at(b)] -= prod[
-                                    TILE * p : TILE * (p + 1), TILE * q : TILE * (q + 1)
-                                ]
-
+                    apply(i, nt3(yh[left], yl[left], bh[:, :256], bl[:, :256]))
                     return 0
 
                 lax.fori_loop(0, chunks, blocks, 0)
@@ -603,7 +653,7 @@
     pltpu.make_async_copy(out_ref, out_hbm, out_sem.at[0]).wait()
 
 
-def schur(scal, lh, ll, wh, wl, col_cross, cross, diag, damp):
+def schur(scal, lh, ll, wh, wl, col_cross, cross, recv, damp):
     return pl.pallas_call(
         schur_kernel,
         in_specs=[pl.BlockSpec(memory_space=SMEM), pl.BlockSpec(memory_space=VMEM)]
@@ -620,7 +670,7 @@
             VMEM((1024, 256), BF16),
             VMEM((64 * TILE, TILE), F32),
             VMEM((32 * TILE, TILE), F32),
-            VMEM((NDEV * LEAD, TILE), F32),
+            VMEM((NDEV, LEAD, TILE), F32),
             VMEM((1024, 2048), F32),
             VMEM((1024, 1024), F32),
             VMEM((2048, 1024), F32),
@@ -628,8 +678,8 @@
             VMEM((1024, 1024), BF16),
             VMEM((1024, 1024), BF16),
             VMEM((1024, 1024), BF16),
-            VMEM((256, 256), BF16),
-            VMEM((256, 256), BF16),
+            VMEM((256, 1024), BF16),
+            VMEM((256, 1024), BF16),
             VMEM((TILE, 1024), F32),
             SMEM((24,), jnp.int32),
             SMEM((9,), jnp.int32),
@@ -644,13 +694,13 @@
             flops=20_000_000_000, bytes_accessed=30_000_000, transcendentals=0
         ),
         name="schur",
-    )(scal, damp, lh, ll, wh, wl, col_cross, cross, diag)
+    )(scal, damp, lh, ll, wh, wl, col_cross, cross, recv)
 
 
 def local(pair_list, jacobian, damping):
     row = lax.axis_index("row")
     column = lax.axis_index("col")
-    payload, cross = grams(jacobian, pair_list, damping)
+    payload, cross = grams(jacobian, pair_list.T, damping)
     recv = lax.all_to_all(payload.reshape(NDEV, SLOTS1, TILE), BOTH, 0, 0, tiled=True)
     cross = cross.reshape(4 * TILE, TILE)
     moves = [
@@ -658,12 +708,11 @@
     ]
     moved = lax.ppermute(cross, BOTH, moves)
     row_cross = lax.all_gather(cross, "col", axis=0, tiled=True)
-    payload, diag, index = gather_rows(recv.reshape(NDEV * SLOTS1, TILE))
+    me = (row * NCOL + column).astype(jnp.int32).reshape(1)
+    payload, index = gather_rows(me, recv.reshape(NDEV * SLOTS1, TILE))
     recv = lax.all_to_all(payload.reshape(NDEV, SLOTS2, TILE), BOTH, 0, 0, tiled=True)
-    recv, diag, moved = lax.optimization_barrier((recv, diag, moved))
+    recv, moved = lax.optimization_barrier((recv, moved))
     col_cross = lax.all_gather(moved, "row", axis=0, tiled=True)
-    diag = lax.all_to_all(diag.reshape(NDEV, LEAD, TILE), BOTH, 0, 0, tiled=True)
-    diag = diag.reshape(NDEV * LEAD, TILE)
     lh, ll, wh, wl = factorise(recv.reshape(NDEV * SLOTS2, TILE))
 
     index = index[:, :8].reshape(NDEV * 8)
@@ -674,7 +723,7 @@
             jnp.stack([row, column]).astype(jnp.int32),
         ]
     )
-    return tuple(schur(scal, lh, ll, wh, wl, col_cross, row_cross, diag, damping))
+    return tuple(schur(scal, lh, ll, wh, wl, col_cross, row_cross, recv, damping))
 
 
 def solution(mesh):

time: 212 us -> 203 us (0.958); the launches traced: 211 us -> 200 us
  blocking collectives: 34.7 us -> 0 us
  waiting for transfers between devices: 36.3 us -> 67 us
  Pallas kernels: 99.6 us -> 91.3 us
    all_to_all x1 -> x0, blocking collectives: 34.7 us -> none  [local(): lax.all_to_all(payload.reshape(NDEV, SLOTS1, TILE), BOTH, 0, 0, tiled=True)]
    all_to_all x1, waiting for transfers between devices: 0.01 us -> 24.3 us  [local(): lax.all_to_all(payload.reshape(NDEV, SLOTS1, TILE), BOTH, 0, 0, tiled=True)]
    all_gather x1, waiting for transfers between devices: 1.74 us -> 8.46 us  [local(): col_cross = lax.all_gather(moved, 'row', axis=0, tiled=True)]
    pallas_call x1, Pallas kernels: 45.3 us -> 39.9 us  [schur(): pl.pallas_call(schur_kernel, in_specs=[pl.BlockSpec(memory_space=SMEM), p...]
    pallas_call x1, Pallas kernels: 4.06 us -> 1.13 us  [gather_rows(): pl.pallas_call(gather_kernel, in_specs=[pl.BlockSpec(memory_space=SMEM),...]
  transfers between devices with their start and end apart: 5 -> 5, of which waited for: 2 -> 3; matrix products, arithmetic and copies ran while one was open for 0% -> 0% of each run, Pallas kernels for 23% -> 23%
where the time goes in v1:
time: 203 us; the launch traced here: 200 us
  Pallas kernels  91.3 us (45%)
  waiting for transfers between devices  67 us (33%)
  starting transfers between devices  24 us (12%)
  between operations  14.1 us (7%)
  local copies, waits for them, and re-layouts  2.44 us (1%)
    pallas_call x1, Pallas kernels, factorise(): pl.pallas_call(factor_kernel, in_specs=[pl.BlockSpec(memory_space=VMEM)],...  44.8 us
    pallas_call x1, Pallas kernels, schur(): pl.pallas_call(schur_kernel, in_specs=[pl.BlockSpec(memory_space=SMEM), p...  39.9 us
    ppermute x1, waiting for transfers between devices, local(): moved = lax.ppermute(cross, BOTH, moves)  34.1 us
    all_to_all x1, waiting for transfers between devices, local(): lax.all_to_all(payload.reshape(NDEV, SLOTS1, TILE), BOTH, 0, 0, tiled=True)  24.3 us
    all_to_all x1, starting transfers between devices, local(): lax.all_to_all(payload.reshape(NDEV, SLOTS1, TILE), BOTH, 0, 0, tiled=True)  10.2 us
    all_to_all x1, starting transfers between devices, local(): lax.all_to_all(payload.reshape(NDEV, SLOTS2, TILE), BOTH, 0, 0, tiled=True)  8.99 us
    all_gather x1, waiting for transfers between devices, local(): col_cross = lax.all_gather(moved, 'row', axis=0, tiled=True)  8.46 us
    pallas_call x1, Pallas kernels, grams(): pl.pallas_call(gram_kernel, grid=(4,), in_specs=[pl.BlockSpec((1, 1024, 2...  5.48 us
  transfers between devices with their start and end apart: 5, of which 3 were waited for; matrix products, arithmetic and copies ran while one was open for 0% of the time, Pallas kernels for 23%

profile of v1, /device:TPU:32, one launch (start us, length us, event | category | flops | bytes accessed | tf_op | source)
XLA Modules:
  0.0 199.6 jit_solution(1080017802090839461)
XLA Ops:
  7.2 0.0 all-gather.5.cloned.1.call-start
  7.2 5.5 %grams.1 = (f32[2048,128]{1,0:T(8,128)}, f32[4,128,128]{2,1,0:T(8,128)}) custom-call(f32[4,1024,256]{2,1,0:T(8,128)} %jac_ref.1, s32[2,4]{1,0:T(2,128)} %bitcast.16, f32[1024]{0:T(1024)} %damp_ref.3), custom_call_target="tpu_custom_call" | custom-call | tf_op jit(solution)/shard_map/grams/pallas_call | solution.py:84
  12.7 0.0 all-gather.5.cloned.1.call-update
  12.7 10.2 %all-to-all-start = ((f32[128,16,128]{2,1,0:T(8,128)}), f32[128,16,128]{2,1,0:T(8,128)S(1)}, u32[]{:S(2)}, u32[]{:S(2)}) async-start(f32[128,16,128]{2,1,0:T(8,128)} %bitcast.13), calls=%async_computation | async-start | bytes 2097152 | tf_op jit(solution)/shard_map/all_to_all | solution.py:704
  23.0 24.3 %all-to-all-done = f32[128,16,128]{2,1,0:T(8,128)S(1)} async-done(((f32[128,16,128]{2,1,0:T(8,128)}), f32[128,16,128]{2,1,0:T(8,128)S(1)}, u32[]{:S(2)}, u32[]{:S(2)}) %all-to-all-start) | async-done | bytes 1048608 | tf_op jit(solution)/shard_map/all_to_all | solution.py:704
  47.3 1.1 gather_rows.1
  48.4 0.0 copy-start
  48.4 1.5 copy-done
  49.9 0.0 copy-start.1
  49.9 9.0 %all-to-all-start.1 = ((f32[128,40,128]{2,1,0:T(8,128)}), f32[128,40,128]{2,1,0:T(8,128)}, u32[]{:S(2)}, u32[]{:S(2)}) async-start(f32[128,40,128]{2,1,0:T(8,128)} %bitcast.11), calls=%async_computation.1 | async-start | bytes 5242880 | tf_op jit(solution)/shard_map/all_to_all | solution.py:713
  58.9 0.0 all-gather.3.cloned.1.call-start
  59.0 0.0 copy-done.1
  59.0 4.7 %collective-permute-start = (f32[512,128]{1,0:T(8,128)S(1)}, f32[512,128]{1,0:T(8,128)S(1)}, u32[]{:S(2)}, u32[]{:S(2)}) collective-permute-start(f32[512,128]{1,0:T(8,128)S(1)} %bitcast.15), channel_id=1, source_target_pairs={{0,0},{1,8},{2,16},{3,24},{4,32},{5,40},{6,48},{7,56},{8,64},{9,72... | collective-permute-start | bytes 786440 | tf_op jit(solution)/shard_map/ppermute | solution.py:709
  63.7 34.1 %collective-permute-done = f32[512,128]{1,0:T(8,128)S(1)} collective-permute-done((f32[512,128]{1,0:T(8,128)S(1)}, f32[512,128]{1,0:T(8,128)S(1)}, u32[]{:S(2)}, u32[]{:S(2)}) %collective-permute-start) | collective-permute-done | bytes 262176 | tf_op jit(solution)/shard_map/ppermute | solution.py:709
  97.9 0.0 copy-start.2
  97.9 0.0 all-to-all-done.1.recv_hbm
  97.9 0.7 copy-done.2
  98.6 0.0 all-gather.3.cloned.1.call-update
  98.6 0.1 reshape.28
  98.7 0.1 dynamic_slice.7
  98.8 0.1 dynamic_slice.6
  98.8 0.7 pad_add_fusion.scal_ref
  99.5 44.8 %factorise.1 = (bf16[1024,1024]{1,0:T(8,128)(2,1)}, bf16[1024,1024]{1,0:T(8,128)(2,1)}, bf16[1024,256]{1,0:T(8,128)(2,1)}, bf16[1024,256]{1,0:T(8,128)(2,1)}) custom-call(f32[5120,128]{1,0:T(8,128)} %bitcast.8.recv_ref), custom_call_target="tpu_custom_call" | custom-call | flops 40000000000 | bytes 8000000 | tf_op jit(solution)/shard_map/factorise/pallas_call | solution.py:363
  144.4 0.0 all-gather.5.cloned.1.call-done.cross_hbm
  144.4 8.5 %all-gather.3.cloned.1.call-done.col_hbm = f32[8192,128]{1,0:T(8,128)} async-done(((f32[512,128]{1,0:T(8,128)}), f32[8192,128]{1,0:T(8,128)}) %all-gather.3.cloned.1.call-update) | async-done | bytes 4194320 | tf_op jit(solution)/shard_map/all_gather | solution.py:715
  152.9 39.9 %schur.1 = (f32[1024,1024]{1,0:T(8,128)}, f32[1024,2048]{1,0:T(8,128)}) custom-call(s32[194]{0:T(256)} %pad_add_fusion.scal_ref, f32[1024]{0:T(1024)} %damp_ref.3, bf16[1024,1024]{1,0:T(8,128)(2,1)} %get-tuple-element.17.lh_hbm, bf16[1024,1024]{1,0:T(8,128)(2,1)} %get-tuple-element.18.ll_hbm, bf16[1024,256]{1,0:T(8,128)(2,1)} %get-tuple-element.19.wh_hbm, ...), custom_call_target="tpu_custom_call" | custom-call | flops 20000000000 | bytes 30000000 | tf_op jit(solution)/shard_map/schur/pallas_call | solution.py:657
Async XLA Ops:
  7.2 137.2 %all-gather.5.cloned.1.call-start = ((), (), s32[]{:S(2)}) async-start(), calls=%async_computation.3 | async-start | bytes 2359296 | tf_op jit(solution)/shard_map/all_gather | solution.py:710
  12.7 34.6 %all-to-all-start = ((f32[128,16,128]{2,1,0:T(8,128)}), f32[128,16,128]{2,1,0:T(8,128)S(1)}, u32[]{:S(2)}, u32[]{:S(2)}) async-start(f32[128,16,128]{2,1,0:T(8,128)} %bitcast.13), calls=%async_computation | async-start | bytes 2097152 | tf_op jit(solution)/shard_map/all_to_all | solution.py:704
  48.4 1.5 copy-start
  49.9 9.1 %copy-start.1 = (f32[4,128,128]{2,1,0:T(8,128)S(1)}, f32[4,128,128]{2,1,0:T(8,128)}, u32[]{:S(2)}) copy-start(f32[4,128,128]{2,1,0:T(8,128)} %get-tuple-element.15) | copy-start | bytes 786436
  49.9 47.9 %all-to-all-start.1 = ((f32[128,40,128]{2,1,0:T(8,128)}), f32[128,40,128]{2,1,0:T(8,128)}, u32[]{:S(2)}, u32[]{:S(2)}) async-start(f32[128,40,128]{2,1,0:T(8,128)} %bitcast.11), calls=%async_computation.1 | async-start | bytes 5242880 | tf_op jit(solution)/shard_map/all_to_all | solution.py:713
  58.9 93.9 %all-gather.3.cloned.1.call-start = ((), (), s32[]{:S(2)}) async-start(), calls=%async_computation.2 | async-start | bytes 4456448 | tf_op jit(solution)/shard_map/all_gather | solution.py:715
  59.0 38.9 %collective-permute-start = (f32[512,128]{1,0:T(8,128)S(1)}, f32[512,128]{1,0:T(8,128)S(1)}, u32[]{:S(2)}, u32[]{:S(2)}) collective-permute-start(f32[512,128]{1,0:T(8,128)S(1)} %bitcast.15), channel_id=1, source_target_pairs={{0,0},{1,8},{2,16},{3,24},{4,32},{5,40},{6,48},{7,56},{8,64},{9,72... | collective-permute-start | bytes 786440 | tf_op jit(solution)/shard_map/ppermute | solution.py:709
  97.9 0.7 copy-start.2
Sparse Core Ops, SparseCore 0:
  12.8 34.2 all-gather.4
  98.7 54.0 all-gather.2

commit v2 on v1

--- a/solution.py
+++ b/solution.py
@@ -262,10 +262,46 @@
     return jnp.dot(a, b, precision=HI, preferred_element_type=F32)
 
 
+def mark_rows(scal_ref, where_ref, tiles_ref):
+    row = scal_ref[192]
+    for u in range(LEAD):
+        where_ref[u] = 0
+
+    def mark(p, _):
+        a = scal_ref[2 * p] - LEAD * row
+        where_ref[a] = jnp.where(scal_ref[2 * p + 1] < LEAD, 1, where_ref[a])
+        return 0
+
+    @pl.when(row >= 1)
+    def _():
+        lax.fori_loop(0, 32, mark, 0)
+
+    def place(u, count):
+        used = where_ref[u] == 1
+        where_ref[u] = jnp.where(used, count, -1)
+        tiles_ref[count] = u
+        return count + used.astype(jnp.int32)
+
+    return lax.fori_loop(0, LEAD, place, jnp.int32(0))
+
+
 def factor_kernel(
-    recv_ref, lh_hbm, ll_hbm, wh_hbm, wl_hbm,
-    lh_ref, ll_ref, wh_ref, wl_ref, body, inv_ref, pa, pb, pc, ra, rb, sem,
+    scal_ref, recv_ref, cross_hbm, factor_hbm, yh_hbm, yl_hbm,
+    lh_ref, ll_ref, wh_ref, wl_ref, body, inv_ref, pa, pb, pc, ra, rb,
+    cross_ref, rows, xh, xl, yh, yl, none_ref, where_ref, tiles_ref, load_sem, factor_sem, y_sem,
 ):
+    load = pltpu.make_async_copy(cross_hbm, cross_ref, load_sem.at[0])
+    load.start()
+    row = scal_ref[192]
+    n_row = mark_rows(scal_ref, where_ref, tiles_ref)
+    chunks = (n_row + 1) // 2
+    none_ref[...] = jnp.zeros_like(none_ref)
+
+    def clear(i, _):
+        rows[at(i), :] = jnp.zeros((TILE, 1024), F32)
+        return 0
+
+    lax.fori_loop(0, n_row, clear, 0)
     lane = lax.broadcasted_iota(jnp.int32, (TILE, TILE), 1)
     sub = lax.broadcasted_iota(jnp.int32, (TILE, TILE), 0)
 
@@ -284,11 +320,25 @@
             here = slice(TILE * k, TILE * (k + 1))
             body[here, here] = tile + jnp.where(lane == sub, damp[:, k : k + 1], 0.0)
 
+    load.wait()
+
+    def fill(p, _):
+        a = scal_ref[2 * p] - LEAD * row
+        b = scal_ref[2 * p + 1]
+
+        @pl.when((b < LEAD) & (where_ref[a] >= 0))
+        def _():
+            rows[at(where_ref[a]), at(b)] += cross_ref[at(p), :]
+
+        return 0
+
+    lax.fori_loop(0, 32, fill, 0)
+
     def step(k, _):
-        rows = [
+        groups = [
             body[pl.ds(pl.multiple_of(k * TILE + 8 * v, 8), 8), at(k)] for v in range(16)
         ]
-        upper, inverse = factor128(rows)
+        upper, inverse = factor128(groups)
         inv = jnp.concatenate(inverse, axis=0)
         inv_ref[at(k), :] = inv
         wa, wb = right_stacks(inv)
@@ -332,8 +382,6 @@
         tile = jnp.concatenate(upper, axis=0).T
         body[at(k), at(k)] = tile
         lh_ref[at(k), at(k)], ll_ref[at(k), at(k)] = split(tile)
-        pltpu.make_async_copy(lh_ref.at[:, at(k)], lh_hbm.at[:, at(k)], sem.at[0]).start()
-        pltpu.make_async_copy(ll_ref.at[:, at(k)], ll_hbm.at[:, at(k)], sem.at[1]).start()
         return 0
 
     lax.fori_loop(0, LEAD, step, 0)
@@ -347,177 +395,6 @@
         wh_ref[one, TILE:], wl_ref[one, TILE:] = zero, zero
         wh_ref[two, :TILE], wl_ref[two, :TILE] = split(corner)
         wh_ref[two, TILE:], wl_ref[two, TILE:] = split(inv_ref[two, :])
-    last = [
-        pltpu.make_async_copy(wh_ref, wh_hbm, sem.at[2]),
-        pltpu.make_async_copy(wl_ref, wl_hbm, sem.at[3]),
-    ]
-    for copy in last:
-        copy.start()
-    pltpu.make_async_copy(lh_ref, lh_hbm, sem.at[0]).wait()
-    pltpu.make_async_copy(ll_ref, ll_hbm, sem.at[1]).wait()
-    for copy in last:
-        copy.wait()
-
-
-def factorise(recv):
-    return pl.pallas_call(
-        factor_kernel,
-        in_specs=[pl.BlockSpec(memory_space=VMEM)],
-        out_specs=[pl.BlockSpec(memory_space=pltpu.HBM)] * 4,
-        out_shape=[
-            jax.ShapeDtypeStruct((1024, 1024), BF16),
-            jax.ShapeDtypeStruct((1024, 1024), BF16),
-            jax.ShapeDtypeStruct((1024, 256), BF16),
-            jax.ShapeDtypeStruct((1024, 256), BF16),
-        ],
-        scratch_shapes=[VMEM((1024, 1024), BF16)] * 2
-        + [VMEM((1024, 256), BF16)] * 2
-        + [VMEM((1024, 1024), F32), VMEM((1024, TILE), F32)]
-        + [VMEM((1024, 256), BF16)] * 5
-        + [pltpu.SemaphoreType.DMA((4,))],
-        compiler_params=pltpu.CompilerParams(vmem_limit_bytes=58 * 1024 * 1024),
-        cost_estimate=pl.CostEstimate(
-            flops=40_000_000_000, bytes_accessed=8_000_000, transcendentals=0
-        ),
-        name="factorise",
-    )(recv)
-
-
-def schur_kernel(
-    scal_ref, damp_ref, lh_hbm, ll_hbm, wh_hbm, wl_hbm, col_hbm, cross_hbm, recv_hbm,
-    factor_hbm, out_hbm,
-    lh_ref, ll_ref, wh_ref, wl_ref, col_ref, cross_ref, diag_ref, out_ref, rows, cols,
-    xh, xl, yh, yl, bh, bl, none_ref, where_ref, row_tiles, col_tiles, used_ref,
-    load_sem, factor_sem, out_sem,
-):
-    row = scal_ref[192]
-    column = scal_ref[193]
-    loads = [
-        pltpu.make_async_copy(source, target, load_sem.at[i])
-        for i, (source, target) in enumerate(
-            [
-                (cross_hbm, cross_ref),
-                (col_hbm, col_ref),
-                (recv_hbm.at[:, DAMP_SLOT:SLOTS2], diag_ref),
-                (lh_hbm, lh_ref),
-                (ll_hbm, ll_ref),
-                (wh_hbm, wh_ref),
-                (wl_hbm, wl_ref),
-            ]
-        )
-    ]
-    for copy in loads:
-        copy.start()
-    none_ref[...] = jnp.zeros_like(none_ref)
-    for u in range(24):
-        where_ref[u] = 0
-    for u in range(64):
-        used_ref[u] = 0
-
-    def mark_row(p, _):
-        a = scal_ref[2 * p] - LEAD * row
-        where_ref[a] = jnp.where(scal_ref[2 * p + 1] < LEAD, 1, where_ref[a])
-        return 0
-
-    def mark_col(p, _):
-        tile = scal_ref[64 + 2 * p]
-        a = tile - 16 * column + LEAD
-        b = scal_ref[65 + 2 * p]
-
-        @pl.when((b < LEAD) & (tile >= LEAD) & (tile <= LEAD * row + 7))
-        def _():
-            where_ref[a] = 1
-            used_ref[4 * (a - LEAD) + b // 2] = 1
-
-        return 0
-
-    @pl.when(row >= 1)
-    def _():
-        lax.fori_loop(0, 32, mark_row, 0)
-        lax.fori_loop(0, 64, mark_col, 0)
-
-    def place_row(u, count):
-        used = where_ref[u] == 1
-        where_ref[u] = jnp.where(used, count, -1)
-        row_tiles[count] = u
-        return count + used.astype(jnp.int32)
-
-    def place_col(u, count):
-        used = where_ref[u + LEAD] == 1
-        where_ref[u + LEAD] = jnp.where(used, count, -1)
-        col_tiles[count] = u
-        return count + used.astype(jnp.int32)
-
-    n_row = lax.fori_loop(0, LEAD, place_row, jnp.int32(0))
-    n_col = lax.fori_loop(0, 16, place_col, jnp.int32(0))
-
-    def blank(i, _):
-        out_ref[at(i, 32), :] = jnp.zeros((32, 2048), F32)
-        return 0
-
-    lax.fori_loop(0, 32, blank, 0)
-
-    def clear(i, _):
-        rows[at(i), :] = jnp.zeros((TILE, 1024), F32)
-        return 0
-
-    lax.fori_loop(0, n_row, clear, 0)
-
-    def clear_cols(i, _):
-        cols[at(i), :] = jnp.zeros((TILE, 1024), F32)
-        return 0
-
-    lax.fori_loop(0, n_col, clear_cols, 0)
-    loads[0].wait()
-
-    def fill_row(p, _):
-        a = scal_ref[2 * p] - LEAD * row
-        b = scal_ref[2 * p + 1]
-        here = b - 16 * column
-
-        @pl.when((b < LEAD) & (where_ref[a] >= 0))
-        def _():
-            rows[at(where_ref[a]), at(b)] += cross_ref[at(p), :]
-
-        @pl.when((b >= LEAD) & (here >= 0) & (here < 16))
-        def _():
-            out_ref[at(a), at(here)] += cross_ref[at(p), :]
-
-        return 0
-
-    def fill_col(p, _):
-        a = scal_ref[64 + 2 * p] - 16 * column + LEAD
-        b = scal_ref[65 + 2 * p]
-
-        @pl.when((b < LEAD) & (where_ref[a] >= 0))
-        def _():
-            cols[at(where_ref[a]), at(b)] += col_ref[at(p), :]
-
-        return 0
-
-    lax.fori_loop(0, 32, fill_row, 0)
-    loads[1].wait()
-    lax.fori_loop(0, 64, fill_col, 0)
-    loads[2].wait()
-
-    @pl.when((row >= 1) & (row // 2 == column))
-    def _():
-        lane = lax.broadcasted_iota(jnp.int32, (TILE, TILE), 1)
-        sub = lax.broadcasted_iota(jnp.int32, (TILE, TILE), 0)
-        entries = diag_ref[:, DIAG_SLOT - DAMP_SLOT, :]
-        for u in range(4):
-            mine = jnp.where(lane == LEAD * row + 4 + u, entries, 0.0)
-            pair = diag_ref[:, OWN_SLOT - DAMP_SLOT + u, :]
-            one, two = unpack(pair, jnp.sum(mine, axis=1, keepdims=True))
-            for s, tile in ((u, one), (u + 4, two)):
-                damp = damp_ref[TILE * s : TILE * (s + 1)].reshape(1, TILE)
-                damp = jnp.where(lane == sub, jnp.broadcast_to(damp, (TILE, TILE)), 0.0)
-                out_ref[TILE * s : TILE * (s + 1), at(LEAD * (row % 2) + s)] += tile + damp
-
-    for copy in loads[3:]:
-        copy.wait()
-
-    chunks = (n_row + 1) // 2
     for g in range(4):
         here = slice(256 * g, 256 * (g + 1))
 
@@ -570,9 +447,166 @@
             yh[part, here], yl[part, here] = split(
                 nn3(*split(rest), wh_ref[here, :], wl_ref[here, :])
             )
+            if g == 0:
+                pltpu.make_async_copy(yh.at[part], yh_hbm.at[part], y_sem.at[0]).start()
+                pltpu.make_async_copy(yl.at[part], yl_hbm.at[part], y_sem.at[1]).start()
             return 0
 
         lax.fori_loop(0, chunks, backward, 0)
+
+    def sent(i, _):
+        part = at(i, 256)
+        pltpu.make_async_copy(yh.at[part], yh_hbm.at[part], y_sem.at[0]).wait()
+        pltpu.make_async_copy(yl.at[part], yl_hbm.at[part], y_sem.at[1]).wait()
+        return 0
+
+    lax.fori_loop(0, chunks, sent, 0)
+    pltpu.make_async_copy(rows, factor_hbm, factor_sem.at[0]).wait()
+
+
+def factorise(scal, recv, cross):
+    return pl.pallas_call(
+        factor_kernel,
+        in_specs=[
+            pl.BlockSpec(memory_space=SMEM),
+            pl.BlockSpec(memory_space=VMEM),
+            pl.BlockSpec(memory_space=pltpu.HBM),
+        ],
+        out_specs=[pl.BlockSpec(memory_space=pltpu.HBM)] * 3,
+        out_shape=[
+            jax.ShapeDtypeStruct((1024, 1024), F32),
+            jax.ShapeDtypeStruct((1024, 1024), BF16),
+            jax.ShapeDtypeStruct((1024, 1024), BF16),
+        ],
+        scratch_shapes=[VMEM((1024, 1024), BF16)] * 2
+        + [VMEM((1024, 256), BF16)] * 2
+        + [VMEM((1024, 1024), F32), VMEM((1024, TILE), F32)]
+        + [VMEM((1024, 256), BF16)] * 5
+        + [VMEM((32 * TILE, TILE), F32), VMEM((1024, 1024), F32)]
+        + [VMEM((1024, 1024), BF16)] * 4
+        + [
+            VMEM((TILE, 1024), F32),
+            SMEM((LEAD,), jnp.int32),
+            SMEM((LEAD + 1,), jnp.int32),
+            pltpu.SemaphoreType.DMA((1,)),
+            pltpu.SemaphoreType.DMA((1,)),
+            pltpu.SemaphoreType.DMA((2,)),
+        ],
+        compiler_params=pltpu.CompilerParams(vmem_limit_bytes=59 * 1024 * 1024),
+        cost_estimate=pl.CostEstimate(
+            flops=40_000_000_000, bytes_accessed=8_000_000, transcendentals=0
+        ),
+        name="factorise",
+    )(scal, recv, cross)
+
+
+def schur_kernel(
+    scal_ref, damp_ref, yh_hbm, yl_hbm, col_hbm, cross_hbm, recv_hbm, out_hbm,
+    yh, yl, col_ref, cross_ref, diag_ref, out_ref, cols, bh, bl,
+    row_where, row_tiles, where_ref, col_tiles, used_ref, load_sem, out_sem,
+):
+    row = scal_ref[192]
+    column = scal_ref[193]
+    loads = [
+        pltpu.make_async_copy(source, target, load_sem.at[i])
+        for i, (source, target) in enumerate(
+            [
+                (cross_hbm, cross_ref),
+                (col_hbm, col_ref),
+                (recv_hbm.at[:, DAMP_SLOT:SLOTS2], diag_ref),
+                (yh_hbm, yh),
+                (yl_hbm, yl),
+            ]
+        )
+    ]
+    for copy in loads:
+        copy.start()
+    for u in range(16):
+        where_ref[u] = 0
+    for u in range(64):
+        used_ref[u] = 0
+
+    def mark_col(p, _):
+        tile = scal_ref[64 + 2 * p]
+        a = tile - 16 * column
+        b = scal_ref[65 + 2 * p]
+
+        @pl.when((b < LEAD) & (tile >= LEAD) & (tile <= LEAD * row + 7))
+        def _():
+            where_ref[a] = 1
+            used_ref[4 * a + b // 2] = 1
+
+        return 0
+
+    @pl.when(row >= 1)
+    def _():
+        lax.fori_loop(0, 64, mark_col, 0)
+
+    def place_col(u, count):
+        used = where_ref[u] == 1
+        where_ref[u] = jnp.where(used, count, -1)
+        col_tiles[count] = u
+        return count + used.astype(jnp.int32)
+
+    n_row = mark_rows(scal_ref, row_where, row_tiles)
+    chunks = (n_row + 1) // 2
+    n_col = lax.fori_loop(0, 16, place_col, jnp.int32(0))
+
+    def blank(i, _):
+        out_ref[at(i, 32), :] = jnp.zeros((32, 2048), F32)
+        return 0
+
+    lax.fori_loop(0, 32, blank, 0)
+
+    def clear_cols(i, _):
+        cols[at(i), :] = jnp.zeros((TILE, 1024), F32)
+        return 0
+
+    lax.fori_loop(0, n_col, clear_cols, 0)
+    loads[0].wait()
+
+    def fill_row(p, _):
+        a = scal_ref[2 * p] - LEAD * row
+        b = scal_ref[2 * p + 1]
+        here = b - 16 * column
+
+        @pl.when((b >= LEAD) & (here >= 0) & (here < 16))
+        def _():
+            out_ref[at(a), at(here)] += cross_ref[at(p), :]
+
+        return 0
+
+    def fill_col(p, _):
+        a = scal_ref[64 + 2 * p] - 16 * column
+        b = scal_ref[65 + 2 * p]
+
+        @pl.when((b < LEAD) & (where_ref[a] >= 0))
+        def _():
+            cols[at(where_ref[a]), at(b)] += col_ref[at(p), :]
+
+        return 0
+
+    lax.fori_loop(0, 32, fill_row, 0)
+    loads[1].wait()
+    lax.fori_loop(0, 64, fill_col, 0)
+    loads[2].wait()
+
+    @pl.when((row >= 1) & (row // 2 == column))
+    def _():
+        lane = lax.broadcasted_iota(jnp.int32, (TILE, TILE), 1)
+        sub = lax.broadcasted_iota(jnp.int32, (TILE, TILE), 0)
+        entries = diag_ref[:, DIAG_SLOT - DAMP_SLOT, :]
+        for u in range(4):
+            mine = jnp.where(lane == LEAD * row + 4 + u, entries, 0.0)
+            pair = diag_ref[:, OWN_SLOT - DAMP_SLOT + u, :]
+            one, two = unpack(pair, jnp.sum(mine, axis=1, keepdims=True))
+            for s, tile in ((u, one), (u + 4, two)):
+                damp = damp_ref[TILE * s : TILE * (s + 1)].reshape(1, TILE)
+                damp = jnp.where(lane == sub, jnp.broadcast_to(damp, (TILE, TILE)), 0.0)
+                out_ref[TILE * s : TILE * (s + 1), at(LEAD * (row % 2) + s)] += tile + damp
+
+    for copy in loads[3:]:
+        copy.wait()
 
     def send(c):
         part = at(c)
@@ -649,44 +683,32 @@
         return 0
 
     lax.fori_loop(sent, 16, last, 0)
-    pltpu.make_async_copy(rows, factor_hbm, factor_sem.at[0]).wait()
     pltpu.make_async_copy(out_ref, out_hbm, out_sem.at[0]).wait()
 
 
-def schur(scal, lh, ll, wh, wl, col_cross, cross, recv, damp):
+def schur(scal, yh, yl, col_cross, cross, recv, damp):
     return pl.pallas_call(
         schur_kernel,
         in_specs=[pl.BlockSpec(memory_space=SMEM), pl.BlockSpec(memory_space=VMEM)]
-        + [pl.BlockSpec(memory_space=pltpu.HBM)] * 7,
-        out_specs=[pl.BlockSpec(memory_space=pl.ANY)] * 2,
-        out_shape=[
-            jax.ShapeDtypeStruct((1024, 1024), F32),
-            jax.ShapeDtypeStruct((1024, 2048), F32),
-        ],
+        + [pl.BlockSpec(memory_space=pltpu.HBM)] * 5,
+        out_specs=pl.BlockSpec(memory_space=pltpu.HBM),
+        out_shape=jax.ShapeDtypeStruct((1024, 2048), F32),
         scratch_shapes=[
             VMEM((1024, 1024), BF16),
             VMEM((1024, 1024), BF16),
-            VMEM((1024, 256), BF16),
-            VMEM((1024, 256), BF16),
             VMEM((64 * TILE, TILE), F32),
             VMEM((32 * TILE, TILE), F32),
             VMEM((NDEV, LEAD, TILE), F32),
             VMEM((1024, 2048), F32),
-            VMEM((1024, 1024), F32),
             VMEM((2048, 1024), F32),
-            VMEM((1024, 1024), BF16),
-            VMEM((1024, 1024), BF16),
-            VMEM((1024, 1024), BF16),
-            VMEM((1024, 1024), BF16),
             VMEM((256, 1024), BF16),
             VMEM((256, 1024), BF16),
-            VMEM((TILE, 1024), F32),
-            SMEM((24,), jnp.int32),
-            SMEM((9,), jnp.int32),
+            SMEM((LEAD,), jnp.int32),
+            SMEM((LEAD + 1,), jnp.int32),
+            SMEM((16,), jnp.int32),
             SMEM((17,), jnp.int32),
             SMEM((64,), jnp.int32),
-            pltpu.SemaphoreType.DMA((7,)),
-            pltpu.SemaphoreType.DMA((1,)),
+            pltpu.SemaphoreType.DMA((5,)),
             pltpu.SemaphoreType.DMA((1,)),
         ],
         compiler_params=pltpu.CompilerParams(vmem_limit_bytes=60 * 1024 * 1024),
@@ -694,7 +716,7 @@
             flops=20_000_000_000, bytes_accessed=30_000_000, transcendentals=0
         ),
         name="schur",
-    )(scal, damp, lh, ll, wh, wl, col_cross, cross, recv)
+    )(scal, damp, yh, yl, col_cross, cross, recv)
 
 
 def local(pair_list, jacobian, damping):
@@ -713,7 +735,6 @@
     recv = lax.all_to_all(payload.reshape(NDEV, SLOTS2, TILE), BOTH, 0, 0, tiled=True)
     recv, moved = lax.optimization_barrier((recv, moved))
     col_cross = lax.all_gather(moved, "row", axis=0, tiled=True)
-    lh, ll, wh, wl = factorise(recv.reshape(NDEV * SLOTS2, TILE))
 
     index = index[:, :8].reshape(NDEV * 8)
     scal = jnp.concatenate(
@@ -723,7 +744,8 @@
             jnp.stack([row, column]).astype(jnp.int32),
         ]
     )
-    return tuple(schur(scal, lh, ll, wh, wl, col_cross, row_cross, recv, damping))
+    factor, yh, yl = factorise(scal, recv.reshape(NDEV * SLOTS2, TILE), row_cross)
+    return factor, schur(scal, yh, yl, col_cross, row_cross, recv, damping)
 
 
 def solution(mesh):

time: 203 us -> 195 us (0.961)
  the two profiles are of different devices: /device:TPU:32 before, /device:TPU:9 now
where the time goes in v2:
time: 195 us; the launch traced here: 198 us
  Pallas kernels  97.9 us (50%)
  waiting for transfers between devices  58.8 us (30%)
  starting transfers between devices  24.5 us (13%)
  between operations  14.1 us (7%)
  local copies, waits for them, and re-layouts  2.44 us (1%)
    pallas_call x1, Pallas kernels, factorise(): pl.pallas_call(factor_kernel, in_specs=[pl.BlockSpec(memory_space=SMEM),...  67 us
    ppermute x1, waiting for transfers between devices, local(): moved = lax.ppermute(cross, BOTH, moves)  34.6 us
    pallas_call x1, Pallas kernels, schur(): pl.pallas_call(schur_kernel, in_specs=[pl.BlockSpec(memory_space=SMEM), p...  24.2 us
    all_to_all x1, waiting for transfers between devices, local(): lax.all_to_all(payload.reshape(NDEV, SLOTS1, TILE), BOTH, 0, 0, tiled=True)  24.1 us
    all_to_all x1, starting transfers between devices, local(): lax.all_to_all(payload.reshape(NDEV, SLOTS1, TILE), BOTH, 0, 0, tiled=True)  10.7 us
    all_to_all x1, starting transfers between devices, local(): lax.all_to_all(payload.reshape(NDEV, SLOTS2, TILE), BOTH, 0, 0, tiled=True)  9.2 us
    pallas_call x1, Pallas kernels, grams(): pl.pallas_call(gram_kernel, grid=(4,), in_specs=[pl.BlockSpec((1, 1024, 2...  5.47 us
    ppermute x1, starting transfers between devices, local(): moved = lax.ppermute(cross, BOTH, moves)  4.48 us
  transfers between devices with their start and end apart: 5, of which 2 were waited for; matrix products, arithmetic and copies ran while one was open for 0% of the time, Pallas kernels for 34%

profile of v2, /device:TPU:9, one launch (start us, length us, event | category | flops | bytes accessed | tf_op | source)
XLA Modules:
  0.0 198.3 jit_solution(16715187376437830688)
XLA Ops:
  7.2 0.0 all-gather.3.cloned.1.call-start
  7.2 5.5 %grams.1 = (f32[2048,128]{1,0:T(8,128)}, f32[4,128,128]{2,1,0:T(8,128)}) custom-call(f32[4,1024,256]{2,1,0:T(8,128)} %jac_ref.1, s32[2,4]{1,0:T(2,128)} %bitcast.16, f32[1024]{0:T(1024)} %damp_ref.3), custom_call_target="tpu_custom_call" | custom-call | tf_op jit(solution)/shard_map/grams/pallas_call | solution.py:84
  12.7 0.0 all-gather.3.cloned.1.call-update
  12.7 10.7 %all-to-all-start = ((f32[128,16,128]{2,1,0:T(8,128)}), f32[128,16,128]{2,1,0:T(8,128)S(1)}, u32[]{:S(2)}, u32[]{:S(2)}) async-start(f32[128,16,128]{2,1,0:T(8,128)} %bitcast.13), calls=%async_computation | async-start | bytes 2097152 | tf_op jit(solution)/shard_map/all_to_all | solution.py:726
  23.5 24.1 %all-to-all-done = f32[128,16,128]{2,1,0:T(8,128)S(1)} async-done(((f32[128,16,128]{2,1,0:T(8,128)}), f32[128,16,128]{2,1,0:T(8,128)S(1)}, u32[]{:S(2)}, u32[]{:S(2)}) %all-to-all-start) | async-done | bytes 1048608 | tf_op jit(solution)/shard_map/all_to_all | solution.py:726
  47.5 1.1 gather_rows.1
  48.6 0.0 copy-start
  48.7 1.5 copy-done
  50.1 0.0 copy-start.1
  50.1 9.2 %all-to-all-start.1 = ((f32[128,40,128]{2,1,0:T(8,128)}), f32[128,40,128]{2,1,0:T(8,128)}, u32[]{:S(2)}, u32[]{:S(2)}) async-start(f32[128,40,128]{2,1,0:T(8,128)} %bitcast.11), calls=%async_computation.1 | async-start | bytes 5242880 | tf_op jit(solution)/shard_map/all_to_all | solution.py:735
  59.4 0.0 all-gather.5.cloned.1.call-start
  59.4 0.0 copy-done.1
  59.4 4.5 %collective-permute-start = (f32[512,128]{1,0:T(8,128)S(1)}, f32[512,128]{1,0:T(8,128)S(1)}, u32[]{:S(2)}, u32[]{:S(2)}) collective-permute-start(f32[512,128]{1,0:T(8,128)S(1)} %bitcast.15), channel_id=1, source_target_pairs={{0,0},{1,8},{2,16},{3,24},{4,32},{5,40},{6,48},{7,56},{8,64},{9,72... | collective-permute-start | bytes 786440 | tf_op jit(solution)/shard_map/ppermute | solution.py:731
  63.9 34.6 %collective-permute-done = f32[512,128]{1,0:T(8,128)S(1)} collective-permute-done((f32[512,128]{1,0:T(8,128)S(1)}, f32[512,128]{1,0:T(8,128)S(1)}, u32[]{:S(2)}, u32[]{:S(2)}) %collective-permute-start) | collective-permute-done | bytes 262176 | tf_op jit(solution)/shard_map/ppermute | solution.py:731
  98.5 0.0 copy-start.2
  98.5 0.0 all-to-all-done.1.recv_hbm
  98.5 0.7 copy-done.2
  99.3 0.0 all-gather.5.cloned.1.call-update
  99.3 0.1 reshape.28
  99.4 0.1 dynamic_slice.7
  99.4 0.1 dynamic_slice.6
  99.5 0.6 pad_add_fusion.scal_ref
  100.1 0.0 all-gather.3.cloned.1.call-done.cross_hbm
  100.1 67.0 %factorise.1 = (f32[1024,1024]{1,0:T(8,128)}, bf16[1024,1024]{1,0:T(8,128)(2,1)}, bf16[1024,1024]{1,0:T(8,128)(2,1)}) custom-call(s32[194]{0:T(256)} %pad_add_fusion.scal_ref, f32[5120,128]{1,0:T(8,128)} %bitcast.8.recv_ref, f32[4096,128]{1,0:T(8,128)} %all-gather.3.cloned.1.call-done.cross_hbm), custom_call_target="tpu_custom_call" | custom-call | flops 40000000000 | bytes 8000000 | tf_op jit(solution)/shard_map/factorise/pallas_call | solution.py:468
  167.1 0.0 all-gather.5.cloned.1.call-done.col_hbm
  167.2 24.2 %schur.1 = f32[1024,2048]{1,0:T(8,128)} custom-call(s32[194]{0:T(256)} %pad_add_fusion.scal_ref, f32[1024]{0:T(1024)} %damp_ref.3, bf16[1024,1024]{1,0:T(8,128)(2,1)} %get-tuple-element.17.yh_hbm, bf16[1024,1024]{1,0:T(8,128)(2,1)} %get-tuple-element.18.yl_hbm, f32[8192,128]{1,0:T(8,128)} %all-gather.5.cloned.1.call-done.col_hbm, ...), custom_call_target="tpu_custom_call" | custom-call | flops 20000000000 | bytes 30000000 | tf_op jit(solution)/shard_map/schur/pallas_call | solution.py:690
Async XLA Ops:
  7.2 92.9 %all-gather.3.cloned.1.call-start = ((), (), s32[]{:S(2)}) async-start(), calls=%async_computation.2 | async-start | bytes 2359296 | tf_op jit(solution)/shard_map/all_gather | solution.py:732
  12.7 34.8 %all-to-all-start = ((f32[128,16,128]{2,1,0:T(8,128)}), f32[128,16,128]{2,1,0:T(8,128)S(1)}, u32[]{:S(2)}, u32[]{:S(2)}) async-start(f32[128,16,128]{2,1,0:T(8,128)} %bitcast.13), calls=%async_computation | async-start | bytes 2097152 | tf_op jit(solution)/shard_map/all_to_all | solution.py:726
  48.6 1.5 copy-start
  50.1 9.3 %copy-start.1 = (f32[4,128,128]{2,1,0:T(8,128)S(1)}, f32[4,128,128]{2,1,0:T(8,128)}, u32[]{:S(2)}) copy-start(f32[4,128,128]{2,1,0:T(8,128)} %get-tuple-element.14) | copy-start | bytes 786436
  50.1 48.4 %all-to-all-start.1 = ((f32[128,40,128]{2,1,0:T(8,128)}), f32[128,40,128]{2,1,0:T(8,128)}, u32[]{:S(2)}, u32[]{:S(2)}) async-start(f32[128,40,128]{2,1,0:T(8,128)} %bitcast.11), calls=%async_computation.1 | async-start | bytes 5242880 | tf_op jit(solution)/shard_map/all_to_all | solution.py:735
  59.4 107.8 %all-gather.5.cloned.1.call-start = ((), (), s32[]{:S(2)}) async-start(), calls=%async_computation.3 | async-start | bytes 4456448 | tf_op jit(solution)/shard_map/all_gather | solution.py:737
  59.4 39.1 %collective-permute-start = (f32[512,128]{1,0:T(8,128)S(1)}, f32[512,128]{1,0:T(8,128)S(1)}, u32[]{:S(2)}, u32[]{:S(2)}) collective-permute-start(f32[512,128]{1,0:T(8,128)S(1)} %bitcast.15), channel_id=1, source_target_pairs={{0,0},{1,8},{2,16},{3,24},{4,32},{5,40},{6,48},{7,56},{8,64},{9,72... | collective-permute-start | bytes 786440 | tf_op jit(solution)/shard_map/ppermute | solution.py:731
  98.5 0.7 copy-start.2
Sparse Core Ops, SparseCore 0:
  12.8 34.7 all-gather.2
  99.4 53.7 all-gather.4

commit v3 on v2

--- a/solution.py
+++ b/solution.py
@@ -1,3 +1,5 @@
+import functools
+
 import jax
 import jax.numpy as jnp
 from jax import lax
@@ -295,6 +297,7 @@
     row = scal_ref[192]
     n_row = mark_rows(scal_ref, where_ref, tiles_ref)
     chunks = (n_row + 1) // 2
+    fours = (n_row + 1) // 4
     none_ref[...] = jnp.zeros_like(none_ref)
 
     def clear(i, _):
@@ -398,8 +401,8 @@
     for g in range(4):
         here = slice(256 * g, 256 * (g + 1))
 
-        def forward(i, _, g=g, here=here):
-            part = at(i, 256)
+        def forward(i, _, g=g, here=here, size=512):
+            part = at(i, size)
             rest = rows[part, here]
             if g:
                 rest = rest - nt3(
@@ -413,7 +416,8 @@
             xh[part, here], xl[part, here] = split(x)
             return 0
 
-        lax.fori_loop(0, chunks, forward, 0)
+        lax.fori_loop(0, fours, forward, 0)
+        lax.fori_loop(2 * fours, chunks, functools.partial(forward, size=256), 0)
 
     for s in range(LEAD):
         part = slice(TILE * s, TILE * (s + 1))
@@ -436,8 +440,8 @@
     for g in reversed(range(4)):
         here = slice(256 * g, 256 * (g + 1))
 
-        def backward(i, _, g=g, here=here):
-            part = at(i, 256)
+        def backward(i, _, g=g, here=here, size=512):
+            part = at(i, size)
             rest = rows[part, here]
             if g < 3:
                 past = slice(256 * (g + 1), 1024)
@@ -452,7 +456,8 @@
                 pltpu.make_async_copy(yl.at[part], yl_hbm.at[part], y_sem.at[1]).start()
             return 0
 
-        lax.fori_loop(0, chunks, backward, 0)
+        lax.fori_loop(0, fours, backward, 0)
+        lax.fori_loop(2 * fours, chunks, functools.partial(backward, size=256), 0)
 
     def sent(i, _):
         part = at(i, 256)
@@ -632,6 +637,10 @@
                             TILE * p : TILE * (p + 1), TILE * q : TILE * (q + 1)
                         ]
 
+        def below(i):
+            a = row_tiles[jnp.minimum(2 * i + 1, n_row - 1)]
+            return LEAD * row + a >= 16 * column + one_tile
+
         def used(c):
             return used_ref[4 * one_tile + c] | used_ref[4 * two_tile + c]
 
@@ -646,8 +655,11 @@
             lax.fori_loop(0, 4, prepare, 0)
 
             def blocks(i, _):
-                left = at(i, 256)
-                apply(i, nt3(yh[left, :], yl[left, :], bh[...], bl[...]))
+                @pl.when(below(i))
+                def _():
+                    left = at(i, 256)
+                    apply(i, nt3(yh[left, :], yl[left, :], bh[...], bl[...]))
+
                 return 0
 
             lax.fori_loop(0, chunks, blocks, 0)
@@ -658,8 +670,11 @@
                 bh[:, :256], bl[:, :256] = split(cols[at(j, 256), at(c, 256)])
 
                 def blocks(i, _):
-                    left = (at(i, 256), at(c, 256))
-                    apply(i, nt3(yh[left], yl[left], bh[:, :256], bl[:, :256]))
+                    @pl.when(below(i))
+                    def _():
+                        left = (at(i, 256), at(c, 256))
+                        apply(i, nt3(yh[left], yl[left], bh[:, :256], bl[:, :256]))
+
                     return 0
 
                 lax.fori_loop(0, chunks, blocks, 0)

time: 195 us -> 186 us (0.954)
  the two profiles are of different devices: /device:TPU:9 before, /device:TPU:97 now
where the time goes in v3:
time: 186 us
  Pallas kernels  86.9 us (47%)
  waiting for transfers between devices  57.8 us (31%)
  starting transfers between devices  23.9 us (13%)
  between operations  14.1 us (8%)
  local copies, waits for them, and re-layouts  2.44 us (1%)
    pallas_call x1, Pallas kernels, factorise(): pl.pallas_call(factor_kernel, in_specs=[pl.BlockSpec(memory_space=SMEM),...  59.6 us
    ppermute x1, waiting for transfers between devices, local(): moved = lax.ppermute(cross, BOTH, moves)  33 us
    all_to_all x1, waiting for transfers between devices, local(): lax.all_to_all(payload.reshape(NDEV, SLOTS1, TILE), BOTH, 0, 0, tiled=True)  24.7 us
    pallas_call x1, Pallas kernels, schur(): pl.pallas_call(schur_kernel, in_specs=[pl.BlockSpec(memory_space=SMEM), p...  20.6 us
    all_to_all x1, starting transfers between devices, local(): lax.all_to_all(payload.reshape(NDEV, SLOTS1, TILE), BOTH, 0, 0, tiled=True)  10.1 us
    all_to_all x1, starting transfers between devices, local(): lax.all_to_all(payload.reshape(NDEV, SLOTS2, TILE), BOTH, 0, 0, tiled=True)  8.6 us
    pallas_call x1, Pallas kernels, grams(): pl.pallas_call(gram_kernel, grid=(4,), in_specs=[pl.BlockSpec((1, 1024, 2...  5.48 us
    ppermute x1, starting transfers between devices, local(): moved = lax.ppermute(cross, BOTH, moves)  5.09 us
  transfers between devices with their start and end apart: 5, of which 2 were waited for; matrix products, arithmetic and copies ran while one was open for 0% of the time, Pallas kernels for 33%

profile of v3, /device:TPU:97, one launch (start us, length us, event | category | flops | bytes accessed | tf_op | source)
XLA Modules:
  0.0 185.8 jit_solution(7273498964260850247)
XLA Ops:
  7.2 0.0 all-gather.3.cloned.1.call-start
  7.2 5.5 %grams.1 = (f32[2048,128]{1,0:T(8,128)}, f32[4,128,128]{2,1,0:T(8,128)}) custom-call(f32[4,1024,256]{2,1,0:T(8,128)} %jac_ref.1, s32[2,4]{1,0:T(2,128)} %bitcast.16, f32[1024]{0:T(1024)} %damp_ref.3), custom_call_target="tpu_custom_call" | custom-call | tf_op jit(solution)/shard_map/grams/pallas_call | solution.py:86
  12.7 0.0 all-gather.3.cloned.1.call-update
  12.7 10.1 %all-to-all-start = ((f32[128,16,128]{2,1,0:T(8,128)}), f32[128,16,128]{2,1,0:T(8,128)S(1)}, u32[]{:S(2)}, u32[]{:S(2)}) async-start(f32[128,16,128]{2,1,0:T(8,128)} %bitcast.13), calls=%async_computation | async-start | bytes 2097152 | tf_op jit(solution)/shard_map/all_to_all | solution.py:741
  22.9 24.7 %all-to-all-done = f32[128,16,128]{2,1,0:T(8,128)S(1)} async-done(((f32[128,16,128]{2,1,0:T(8,128)}), f32[128,16,128]{2,1,0:T(8,128)S(1)}, u32[]{:S(2)}, u32[]{:S(2)}) %all-to-all-start) | async-done | bytes 1048608 | tf_op jit(solution)/shard_map/all_to_all | solution.py:741
  47.6 1.1 gather_rows.1
  48.7 0.0 copy-start
  48.8 1.5 copy-done
  50.2 0.0 copy-start.1
  50.2 8.6 %all-to-all-start.1 = ((f32[128,40,128]{2,1,0:T(8,128)}), f32[128,40,128]{2,1,0:T(8,128)}, u32[]{:S(2)}, u32[]{:S(2)}) async-start(f32[128,40,128]{2,1,0:T(8,128)} %bitcast.11), calls=%async_computation.1 | async-start | bytes 5242880 | tf_op jit(solution)/shard_map/all_to_all | solution.py:750
  58.9 0.0 all-gather.5.cloned.1.call-start
  58.9 0.0 copy-done.1
  58.9 5.1 %collective-permute-start = (f32[512,128]{1,0:T(8,128)S(1)}, f32[512,128]{1,0:T(8,128)S(1)}, u32[]{:S(2)}, u32[]{:S(2)}) collective-permute-start(f32[512,128]{1,0:T(8,128)S(1)} %bitcast.15), channel_id=1, source_target_pairs={{0,0},{1,8},{2,16},{3,24},{4,32},{5,40},{6,48},{7,56},{8,64},{9,72... | collective-permute-start | bytes 786440 | tf_op jit(solution)/shard_map/ppermute | solution.py:746
  64.0 33.0 %collective-permute-done = f32[512,128]{1,0:T(8,128)S(1)} collective-permute-done((f32[512,128]{1,0:T(8,128)S(1)}, f32[512,128]{1,0:T(8,128)S(1)}, u32[]{:S(2)}, u32[]{:S(2)}) %collective-permute-start) | collective-permute-done | bytes 262176 | tf_op jit(solution)/shard_map/ppermute | solution.py:746
  97.0 0.0 copy-start.2
  97.1 0.0 all-to-all-done.1.recv_hbm
  97.1 0.7 copy-done.2
  97.8 0.0 all-gather.5.cloned.1.call-update
  97.8 0.1 reshape.28
  97.9 0.1 dynamic_slice.7
  98.0 0.1 dynamic_slice.6
  98.0 0.6 pad_add_fusion.scal_ref
  98.6 0.0 all-gather.3.cloned.1.call-done.cross_hbm
  98.6 59.6 %factorise.1 = (f32[1024,1024]{1,0:T(8,128)}, bf16[1024,1024]{1,0:T(8,128)(2,1)}, bf16[1024,1024]{1,0:T(8,128)(2,1)}) custom-call(s32[194]{0:T(256)} %pad_add_fusion.scal_ref, f32[5120,128]{1,0:T(8,128)} %bitcast.8.recv_ref, f32[4096,128]{1,0:T(8,128)} %all-gather.3.cloned.1.call-done.cross_hbm), custom_call_target="tpu_custom_call" | custom-call | flops 40000000000 | bytes 8000000 | tf_op jit(solution)/shard_map/factorise/pallas_call | solution.py:473
  158.3 0.0 all-gather.5.cloned.1.call-done.col_hbm
  158.3 20.6 %schur.1 = f32[1024,2048]{1,0:T(8,128)} custom-call(s32[194]{0:T(256)} %pad_add_fusion.scal_ref, f32[1024]{0:T(1024)} %damp_ref.3, bf16[1024,1024]{1,0:T(8,128)(2,1)} %get-tuple-element.17.yh_hbm, bf16[1024,1024]{1,0:T(8,128)(2,1)} %get-tuple-element.18.yl_hbm, f32[8192,128]{1,0:T(8,128)} %all-gather.5.cloned.1.call-done.col_hbm, ...), custom_call_target="tpu_custom_call" | custom-call | flops 20000000000 | bytes 30000000 | tf_op jit(solution)/shard_map/schur/pallas_call | solution.py:705
Async XLA Ops:
  7.2 91.5 %all-gather.3.cloned.1.call-start = ((), (), s32[]{:S(2)}) async-start(), calls=%async_computation.2 | async-start | bytes 2359296 | tf_op jit(solution)/shard_map/all_gather | solution.py:747
  12.7 34.9 %all-to-all-start = ((f32[128,16,128]{2,1,0:T(8,128)}), f32[128,16,128]{2,1,0:T(8,128)S(1)}, u32[]{:S(2)}, u32[]{:S(2)}) async-start(f32[128,16,128]{2,1,0:T(8,128)} %bitcast.13), calls=%async_computation | async-start | bytes 2097152 | tf_op jit(solution)/shard_map/all_to_all | solution.py:741
  48.7 1.5 copy-start
  50.2 8.7 %copy-start.1 = (f32[4,128,128]{2,1,0:T(8,128)S(1)}, f32[4,128,128]{2,1,0:T(8,128)}, u32[]{:S(2)}) copy-start(f32[4,128,128]{2,1,0:T(8,128)} %get-tuple-element.14) | copy-start | bytes 786436
  50.2 46.8 %all-to-all-start.1 = ((f32[128,40,128]{2,1,0:T(8,128)}), f32[128,40,128]{2,1,0:T(8,128)}, u32[]{:S(2)}, u32[]{:S(2)}) async-start(f32[128,40,128]{2,1,0:T(8,128)} %bitcast.11), calls=%async_computation.1 | async-start | bytes 5242880 | tf_op jit(solution)/shard_map/all_to_all | solution.py:750
  58.9 99.4 %all-gather.5.cloned.1.call-start = ((), (), s32[]{:S(2)}) async-start(), calls=%async_computation.3 | async-start | bytes 4456448 | tf_op jit(solution)/shard_map/all_gather | solution.py:752
  58.9 38.1 %collective-permute-start = (f32[512,128]{1,0:T(8,128)S(1)}, f32[512,128]{1,0:T(8,128)S(1)}, u32[]{:S(2)}, u32[]{:S(2)}) collective-permute-start(f32[512,128]{1,0:T(8,128)S(1)} %bitcast.15), channel_id=1, source_target_pairs={{0,0},{1,8},{2,16},{3,24},{4,32},{5,40},{6,48},{7,56},{8,64},{9,72... | collective-permute-start | bytes 786440 | tf_op jit(solution)/shard_map/ppermute | solution.py:746
  97.0 0.7 copy-start.2
Sparse Core Ops, SparseCore 0:
  12.8 34.1 all-gather.2
  97.9 54.0 all-gather.4

commit v4 on v3

--- a/solution.py
+++ b/solution.py
@@ -260,10 +260,6 @@
     return one, high + high.T + jnp.where(lane == sub, entries, 0.0)
 
 
-def nn(a, b):
-    return jnp.dot(a, b, precision=HI, preferred_element_type=F32)
-
-
 def mark_rows(scal_ref, where_ref, tiles_ref):
     row = scal_ref[192]
     for u in range(LEAD):
@@ -336,11 +332,20 @@
         return 0
 
     lax.fori_loop(0, 32, fill, 0)
+    for ref in (pa, pb, pc, ra, rb):
+        ref[...] = jnp.zeros_like(ref)
 
     def step(k, _):
         groups = [
             body[pl.ds(pl.multiple_of(k * TILE + 8 * v, 8), 8), at(k)] for v in range(16)
         ]
+        for j in range(2, 4):
+            part = slice(256 * j, 1024)
+            wide = slice(256 * j, 256 * (j + 1))
+            later = j > k // 2
+            wa = jnp.where(later, ra[wide, :], jnp.zeros_like(ra[wide, :]))
+            wb = jnp.where(later, rb[wide, :], jnp.zeros_like(rb[wide, :]))
+            body[part, wide] -= six(pa[part, :], pb[part, :], pc[part, :], wa, wb)
         upper, inverse = factor128(groups)
         inv = jnp.concatenate(inverse, axis=0)
         inv_ref[at(k), :] = inv
@@ -381,7 +386,7 @@
             lax.fori_loop((j >= 2).astype(jnp.int32), 2, rows_of, 0)
             return 0
 
-        lax.fori_loop((k + 1) // 2, 4, update, 0)
+        lax.fori_loop((k + 1) // 2, jnp.minimum(jnp.maximum((k + 3) // 2, 2), 4), update, 0)
         tile = jnp.concatenate(upper, axis=0).T
         body[at(k), at(k)] = tile
         lh_ref[at(k), at(k)], ll_ref[at(k), at(k)] = split(tile)
@@ -391,13 +396,14 @@
     for g in range(4):
         one = slice(256 * g, 256 * g + TILE)
         two = slice(256 * g + TILE, 256 * g + 256)
-        cross = lh_ref[two, one].astype(F32) + ll_ref[two, one].astype(F32)
-        corner = -nn(inv_ref[two, :], nn(cross, inv_ref[one, :]))
-        wh_ref[one, :TILE], wl_ref[one, :TILE] = split(inv_ref[one, :])
+        w1, w2 = split(inv_ref[one, :]), split(inv_ref[two, :])
+        inner = split(nn3(lh_ref[two, one], ll_ref[two, one], *w1))
+        corner = -nn3(*w2, *inner)
+        wh_ref[one, :TILE], wl_ref[one, :TILE] = w1
         zero = jnp.zeros((TILE, TILE), BF16)
         wh_ref[one, TILE:], wl_ref[one, TILE:] = zero, zero
         wh_ref[two, :TILE], wl_ref[two, :TILE] = split(corner)
-        wh_ref[two, TILE:], wl_ref[two, TILE:] = split(inv_ref[two, :])
+        wh_ref[two, TILE:], wl_ref[two, TILE:] = w2
     for g in range(4):
         here = slice(256 * g, 256 * (g + 1))
 

time: 186 us -> 185 us (level)
  the two profiles are of different devices: /device:TPU:97 before, /device:TPU:9 now
where the time goes in v4:
time: 185 us
  Pallas kernels  84.3 us (46%)
  waiting for transfers between devices  58.8 us (32%)
  starting transfers between devices  24.5 us (13%)
  between operations  14.1 us (8%)
  local copies, waits for them, and re-layouts  2.44 us (1%)
    pallas_call x1, Pallas kernels, factorise(): pl.pallas_call(factor_kernel, in_specs=[pl.BlockSpec(memory_space=SMEM),...  57.3 us
    ppermute x1, waiting for transfers between devices, local(): moved = lax.ppermute(cross, BOTH, moves)  34.6 us
    all_to_all x1, waiting for transfers between devices, local(): lax.all_to_all(payload.reshape(NDEV, SLOTS1, TILE), BOTH, 0, 0, tiled=True)  24.1 us
    pallas_call x1, Pallas kernels, schur(): pl.pallas_call(schur_kernel, in_specs=[pl.BlockSpec(memory_space=SMEM), p...  20.5 us
    all_to_all x1, starting transfers between devices, local(): lax.all_to_all(payload.reshape(NDEV, SLOTS1, TILE), BOTH, 0, 0, tiled=True)  10.7 us
    all_to_all x1, starting transfers between devices, local(): lax.all_to_all(payload.reshape(NDEV, SLOTS2, TILE), BOTH, 0, 0, tiled=True)  9.2 us
    pallas_call x1, Pallas kernels, grams(): pl.pallas_call(gram_kernel, grid=(4,), in_specs=[pl.BlockSpec((1, 1024, 2...  5.48 us
    ppermute x1, starting transfers between devices, local(): moved = lax.ppermute(cross, BOTH, moves)  4.48 us
  transfers between devices with their start and end apart: 5, of which 2 were waited for; matrix products, arithmetic and copies ran while one was open for 0% of the time, Pallas kernels for 32%

profile of v4, /device:TPU:9, one launch (start us, length us, event | category | flops | bytes accessed | tf_op | source)
XLA Modules:
  0.0 184.8 jit_solution(13814540158309644842)
XLA Ops:
  7.2 0.0 all-gather.3.cloned.1.call-start
  7.2 5.5 %grams.1 = (f32[2048,128]{1,0:T(8,128)}, f32[4,128,128]{2,1,0:T(8,128)}) custom-call(f32[4,1024,256]{2,1,0:T(8,128)} %jac_ref.1, s32[2,4]{1,0:T(2,128)} %bitcast.16, f32[1024]{0:T(1024)} %damp_ref.3), custom_call_target="tpu_custom_call" | custom-call | tf_op jit(solution)/shard_map/grams/pallas_call | solution.py:86
  12.7 0.0 all-gather.3.cloned.1.call-update
  12.7 10.7 %all-to-all-start = ((f32[128,16,128]{2,1,0:T(8,128)}), f32[128,16,128]{2,1,0:T(8,128)S(1)}, u32[]{:S(2)}, u32[]{:S(2)}) async-start(f32[128,16,128]{2,1,0:T(8,128)} %bitcast.13), calls=%async_computation | async-start | bytes 2097152 | tf_op jit(solution)/shard_map/all_to_all | solution.py:747
  23.5 24.1 %all-to-all-done = f32[128,16,128]{2,1,0:T(8,128)S(1)} async-done(((f32[128,16,128]{2,1,0:T(8,128)}), f32[128,16,128]{2,1,0:T(8,128)S(1)}, u32[]{:S(2)}, u32[]{:S(2)}) %all-to-all-start) | async-done | bytes 1048608 | tf_op jit(solution)/shard_map/all_to_all | solution.py:747
  47.5 1.1 gather_rows.1
  48.7 0.0 copy-start
  48.7 1.5 copy-done
  50.1 0.0 copy-start.1
  50.2 9.2 %all-to-all-start.1 = ((f32[128,40,128]{2,1,0:T(8,128)}), f32[128,40,128]{2,1,0:T(8,128)}, u32[]{:S(2)}, u32[]{:S(2)}) async-start(f32[128,40,128]{2,1,0:T(8,128)} %bitcast.11), calls=%async_computation.1 | async-start | bytes 5242880 | tf_op jit(solution)/shard_map/all_to_all | solution.py:756
  59.4 0.0 all-gather.5.cloned.1.call-start
  59.4 0.0 copy-done.1
  59.4 4.5 %collective-permute-start = (f32[512,128]{1,0:T(8,128)S(1)}, f32[512,128]{1,0:T(8,128)S(1)}, u32[]{:S(2)}, u32[]{:S(2)}) collective-permute-start(f32[512,128]{1,0:T(8,128)S(1)} %bitcast.15), channel_id=1, source_target_pairs={{0,0},{1,8},{2,16},{3,24},{4,32},{5,40},{6,48},{7,56},{8,64},{9,72... | collective-permute-start | bytes 786440 | tf_op jit(solution)/shard_map/ppermute | solution.py:752
  63.9 34.6 %collective-permute-done = f32[512,128]{1,0:T(8,128)S(1)} collective-permute-done((f32[512,128]{1,0:T(8,128)S(1)}, f32[512,128]{1,0:T(8,128)S(1)}, u32[]{:S(2)}, u32[]{:S(2)}) %collective-permute-start) | collective-permute-done | bytes 262176 | tf_op jit(solution)/shard_map/ppermute | solution.py:752
  98.5 0.0 copy-start.2
  98.6 0.0 all-to-all-done.1.recv_hbm
  98.6 0.7 copy-done.2
  99.3 0.0 all-gather.5.cloned.1.call-update
  99.3 0.1 reshape.28
  99.4 0.1 dynamic_slice.7
  99.5 0.1 dynamic_slice.6
  99.5 0.6 pad_add_fusion.scal_ref
  100.1 0.0 all-gather.3.cloned.1.call-done.cross_hbm
  100.1 57.3 %factorise.1 = (f32[1024,1024]{1,0:T(8,128)}, bf16[1024,1024]{1,0:T(8,128)(2,1)}, bf16[1024,1024]{1,0:T(8,128)(2,1)}) custom-call(s32[194]{0:T(256)} %pad_add_fusion.scal_ref, f32[5120,128]{1,0:T(8,128)} %bitcast.8.recv_ref, f32[4096,128]{1,0:T(8,128)} %all-gather.3.cloned.1.call-done.cross_hbm), custom_call_target="tpu_custom_call" | custom-call | flops 40000000000 | bytes 8000000 | tf_op jit(solution)/shard_map/factorise/pallas_call | solution.py:479
  157.4 0.0 all-gather.5.cloned.1.call-done.col_hbm
  157.4 20.5 %schur.1 = f32[1024,2048]{1,0:T(8,128)} custom-call(s32[194]{0:T(256)} %pad_add_fusion.scal_ref, f32[1024]{0:T(1024)} %damp_ref.3, bf16[1024,1024]{1,0:T(8,128)(2,1)} %get-tuple-element.17.yh_hbm, bf16[1024,1024]{1,0:T(8,128)(2,1)} %get-tuple-element.18.yl_hbm, f32[8192,128]{1,0:T(8,128)} %all-gather.5.cloned.1.call-done.col_hbm, ...), custom_call_target="tpu_custom_call" | custom-call | flops 20000000000 | bytes 30000000 | tf_op jit(solution)/shard_map/schur/pallas_call | solution.py:711
Async XLA Ops:
  7.2 93.0 %all-gather.3.cloned.1.call-start = ((), (), s32[]{:S(2)}) async-start(), calls=%async_computation.2 | async-start | bytes 2359296 | tf_op jit(solution)/shard_map/all_gather | solution.py:753
  12.7 34.8 %all-to-all-start = ((f32[128,16,128]{2,1,0:T(8,128)}), f32[128,16,128]{2,1,0:T(8,128)S(1)}, u32[]{:S(2)}, u32[]{:S(2)}) async-start(f32[128,16,128]{2,1,0:T(8,128)} %bitcast.13), calls=%async_computation | async-start | bytes 2097152 | tf_op jit(solution)/shard_map/all_to_all | solution.py:747
  48.7 1.5 copy-start
  50.1 9.3 %copy-start.1 = (f32[4,128,128]{2,1,0:T(8,128)S(1)}, f32[4,128,128]{2,1,0:T(8,128)}, u32[]{:S(2)}) copy-start(f32[4,128,128]{2,1,0:T(8,128)} %get-tuple-element.14) | copy-start | bytes 786436
  50.2 48.4 %all-to-all-start.1 = ((f32[128,40,128]{2,1,0:T(8,128)}), f32[128,40,128]{2,1,0:T(8,128)}, u32[]{:S(2)}, u32[]{:S(2)}) async-start(f32[128,40,128]{2,1,0:T(8,128)} %bitcast.11), calls=%async_computation.1 | async-start | bytes 5242880 | tf_op jit(solution)/shard_map/all_to_all | solution.py:756
  59.4 98.1 %all-gather.5.cloned.1.call-start = ((), (), s32[]{:S(2)}) async-start(), calls=%async_computation.3 | async-start | bytes 4456448 | tf_op jit(solution)/shard_map/all_gather | solution.py:758
  59.4 39.1 %collective-permute-start = (f32[512,128]{1,0:T(8,128)S(1)}, f32[512,128]{1,0:T(8,128)S(1)}, u32[]{:S(2)}, u32[]{:S(2)}) collective-permute-start(f32[512,128]{1,0:T(8,128)S(1)} %bitcast.15), channel_id=1, source_target_pairs={{0,0},{1,8},{2,16},{3,24},{4,32},{5,40},{6,48},{7,56},{8,64},{9,72... | collective-permute-start | bytes 786440 | tf_op jit(solution)/shard_map/ppermute | solution.py:752
  98.5 0.7 copy-start.2
Sparse Core Ops, SparseCore 0:
  12.8 34.7 all-gather.2
  99.4 53.6 all-gather.4

commit v5 on v4

--- a/solution.py
+++ b/solution.py
@@ -514,7 +514,7 @@
 def schur_kernel(
     scal_ref, damp_ref, yh_hbm, yl_hbm, col_hbm, cross_hbm, recv_hbm, out_hbm,
     yh, yl, col_ref, cross_ref, diag_ref, out_ref, cols, bh, bl,
-    row_where, row_tiles, where_ref, col_tiles, used_ref, load_sem, out_sem,
+    row_where, row_tiles, where_ref, col_tiles, used_ref, chunk_ref, load_sem, out_sem,
 ):
     row = scal_ref[192]
     column = scal_ref[193]
@@ -650,44 +650,34 @@
         def used(c):
             return used_ref[4 * one_tile + c] | used_ref[4 * two_tile + c]
 
-        filled = used(0) + used(1) + used(2) + used(3)
-
-        @pl.when(filled > 1)
-        def _():
-            def prepare(c, _):
-                bh[:, at(c, 256)], bl[:, at(c, 256)] = split(cols[at(j, 256), at(c, 256)])
-                return 0
-
-            lax.fori_loop(0, 4, prepare, 0)
-
-            def blocks(i, _):
-                @pl.when(below(i))
-                def _():
-                    left = at(i, 256)
-                    apply(i, nt3(yh[left, :], yl[left, :], bh[...], bl[...]))
-
-                return 0
-
-            lax.fori_loop(0, chunks, blocks, 0)
-
-        def chunk(c, _):
-            @pl.when((filled == 1) & (used(c) == 1))
-            def _():
-                bh[:, :256], bl[:, :256] = split(cols[at(j, 256), at(c, 256)])
+        filled = jnp.int32(0)
+        for c in range(4):
+
+            @pl.when(used(c) == 1)
+            def _(c=c, filled=filled):
+                chunk_ref[filled] = c
+                part = at(filled, 256)
+                bh[:, part], bl[:, part] = split(cols[at(j, 256), 256 * c : 256 * (c + 1)])
+
+            filled = filled + used(c)
+        for depth in range(1, 5):
+
+            @pl.when(filled == depth)
+            def _(depth=depth):
+                wide = slice(0, 256 * depth)
 
                 def blocks(i, _):
                     @pl.when(below(i))
                     def _():
-                        left = (at(i, 256), at(c, 256))
-                        apply(i, nt3(yh[left], yl[left], bh[:, :256], bl[:, :256]))
+                        picks = [at(chunk_ref[f], 256) for f in range(depth)]
+                        high = jnp.concatenate([yh[at(i, 256), p] for p in picks], axis=1)
+                        low = jnp.concatenate([yl[at(i, 256), p] for p in picks], axis=1)
+                        apply(i, nt3(high, low, bh[:, wide], bl[:, wide]))
 
                     return 0
 
                 lax.fori_loop(0, chunks, blocks, 0)
 
-            return 0
-
-        lax.fori_loop(0, 4, chunk, 0)
         done = two_tile + 1
 
         def one(c, _):
@@ -729,6 +719,7 @@
             SMEM((16,), jnp.int32),
             SMEM((17,), jnp.int32),
             SMEM((64,), jnp.int32),
+            SMEM((4,), jnp.int32),
             pltpu.SemaphoreType.DMA((5,)),
             pltpu.SemaphoreType.DMA((1,)),
         ],

time: 185 us -> 188 us (1.016)
  Pallas kernels: 84.3 us -> 88.7 us
    pallas_call x1, Pallas kernels: 57.3 us -> 60.5 us  [factorise(): pl.pallas_call(factor_kernel, in_specs=[pl.BlockSpec(memory_space=SMEM),...]
  transfers between devices with their start and end apart: 5 -> 5, of which waited for: 2 -> 2; matrix products, arithmetic and copies ran while one was open for 0% -> 0% of each run, Pallas kernels for 32% -> 33%
where the time goes in v5:
time: 188 us; the launch traced here: 189 us
  Pallas kernels  88.7 us (47%)
  waiting for transfers between devices  58.8 us (31%)
  starting transfers between devices  24.5 us (13%)
  between operations  14.1 us (8%)
  local copies, waits for them, and re-layouts  2.44 us (1%)
    pallas_call x1, Pallas kernels, factorise(): pl.pallas_call(factor_kernel, in_specs=[pl.BlockSpec(memory_space=SMEM),...  60.5 us
    ppermute x1, waiting for transfers between devices, local(): moved = lax.ppermute(cross, BOTH, moves)  34.6 us
    all_to_all x1, waiting for transfers between devices, local(): lax.all_to_all(payload.reshape(NDEV, SLOTS1, TILE), BOTH, 0, 0, tiled=True)  24.1 us
    pallas_call x1, Pallas kernels, schur(): pl.pallas_call(schur_kernel, in_specs=[pl.BlockSpec(memory_space=SMEM), p...  21.6 us
    all_to_all x1, starting transfers between devices, local(): lax.all_to_all(payload.reshape(NDEV, SLOTS1, TILE), BOTH, 0, 0, tiled=True)  10.7 us
    all_to_all x1, starting transfers between devices, local(): lax.all_to_all(payload.reshape(NDEV, SLOTS2, TILE), BOTH, 0, 0, tiled=True)  9.2 us
    pallas_call x1, Pallas kernels, grams(): pl.pallas_call(gram_kernel, grid=(4,), in_specs=[pl.BlockSpec((1, 1024, 2...  5.48 us
    ppermute x1, starting transfers between devices, local(): moved = lax.ppermute(cross, BOTH, moves)  4.48 us
  transfers between devices with their start and end apart: 5, of which 2 were waited for; matrix products, arithmetic and copies ran while one was open for 0% of the time, Pallas kernels for 33%

profile of v5, /device:TPU:9, one launch (start us, length us, event | category | flops | bytes accessed | tf_op | source)
XLA Modules:
  0.0 189.1 jit_solution(7157410561083593920)
XLA Ops:
  7.2 0.0 all-gather.3.cloned.1.call-start
  7.2 5.5 %grams.1 = (f32[2048,128]{1,0:T(8,128)}, f32[4,128,128]{2,1,0:T(8,128)}) custom-call(f32[4,1024,256]{2,1,0:T(8,128)} %jac_ref.1, s32[2,4]{1,0:T(2,128)} %bitcast.16, f32[1024]{0:T(1024)} %damp_ref.3), custom_call_target="tpu_custom_call" | custom-call | tf_op jit(solution)/shard_map/grams/pallas_call | solution.py:86
  12.7 0.0 all-gather.3.cloned.1.call-update
  12.7 10.7 %all-to-all-start = ((f32[128,16,128]{2,1,0:T(8,128)}), f32[128,16,128]{2,1,0:T(8,128)S(1)}, u32[]{:S(2)}, u32[]{:S(2)}) async-start(f32[128,16,128]{2,1,0:T(8,128)} %bitcast.13), calls=%async_computation | async-start | bytes 2097152 | tf_op jit(solution)/shard_map/all_to_all | solution.py:738
  23.5 24.1 %all-to-all-done = f32[128,16,128]{2,1,0:T(8,128)S(1)} async-done(((f32[128,16,128]{2,1,0:T(8,128)}), f32[128,16,128]{2,1,0:T(8,128)S(1)}, u32[]{:S(2)}, u32[]{:S(2)}) %all-to-all-start) | async-done | bytes 1048608 | tf_op jit(solution)/shard_map/all_to_all | solution.py:738
  47.5 1.1 gather_rows.1
  48.7 0.0 copy-start
  48.7 1.5 copy-done
  50.1 0.0 copy-start.1
  50.2 9.2 %all-to-all-start.1 = ((f32[128,40,128]{2,1,0:T(8,128)}), f32[128,40,128]{2,1,0:T(8,128)}, u32[]{:S(2)}, u32[]{:S(2)}) async-start(f32[128,40,128]{2,1,0:T(8,128)} %bitcast.11), calls=%async_computation.1 | async-start | bytes 5242880 | tf_op jit(solution)/shard_map/all_to_all | solution.py:747
  59.4 0.0 all-gather.5.cloned.1.call-start
  59.4 0.0 copy-done.1
  59.4 4.5 %collective-permute-start = (f32[512,128]{1,0:T(8,128)S(1)}, f32[512,128]{1,0:T(8,128)S(1)}, u32[]{:S(2)}, u32[]{:S(2)}) collective-permute-start(f32[512,128]{1,0:T(8,128)S(1)} %bitcast.15), channel_id=1, source_target_pairs={{0,0},{1,8},{2,16},{3,24},{4,32},{5,40},{6,48},{7,56},{8,64},{9,72... | collective-permute-start | bytes 786440 | tf_op jit(solution)/shard_map/ppermute | solution.py:743
  63.9 34.6 %collective-permute-done = f32[512,128]{1,0:T(8,128)S(1)} collective-permute-done((f32[512,128]{1,0:T(8,128)S(1)}, f32[512,128]{1,0:T(8,128)S(1)}, u32[]{:S(2)}, u32[]{:S(2)}) %collective-permute-start) | collective-permute-done | bytes 262176 | tf_op jit(solution)/shard_map/ppermute | solution.py:743
  98.5 0.0 copy-start.2
  98.6 0.0 all-to-all-done.1.recv_hbm
  98.6 0.7 copy-done.2
  99.3 0.0 all-gather.5.cloned.1.call-update
  99.3 0.1 reshape.28
  99.4 0.1 dynamic_slice.7
  99.5 0.1 dynamic_slice.6
  99.5 0.6 pad_add_fusion.scal_ref
  100.1 0.0 all-gather.3.cloned.1.call-done.cross_hbm
  100.1 60.5 %factorise.1 = (f32[1024,1024]{1,0:T(8,128)}, bf16[1024,1024]{1,0:T(8,128)(2,1)}, bf16[1024,1024]{1,0:T(8,128)(2,1)}) custom-call(s32[194]{0:T(256)} %pad_add_fusion.scal_ref, f32[5120,128]{1,0:T(8,128)} %bitcast.8.recv_ref, f32[4096,128]{1,0:T(8,128)} %all-gather.3.cloned.1.call-done.cross_hbm), custom_call_target="tpu_custom_call" | custom-call | flops 40000000000 | bytes 8000000 | tf_op jit(solution)/shard_map/factorise/pallas_call | solution.py:479
  160.6 0.0 all-gather.5.cloned.1.call-done.col_hbm
  160.6 21.6 %schur.1 = f32[1024,2048]{1,0:T(8,128)} custom-call(s32[194]{0:T(256)} %pad_add_fusion.scal_ref, f32[1024]{0:T(1024)} %damp_ref.3, bf16[1024,1024]{1,0:T(8,128)(2,1)} %get-tuple-element.17.yh_hbm, bf16[1024,1024]{1,0:T(8,128)(2,1)} %get-tuple-element.18.yl_hbm, f32[8192,128]{1,0:T(8,128)} %all-gather.5.cloned.1.call-done.col_hbm, ...), custom_call_target="tpu_custom_call" | custom-call | flops 20000000000 | bytes 30000000 | tf_op jit(solution)/shard_map/schur/pallas_call | solution.py:701
Async XLA Ops:
  7.2 93.0 %all-gather.3.cloned.1.call-start = ((), (), s32[]{:S(2)}) async-start(), calls=%async_computation.2 | async-start | bytes 2359296 | tf_op jit(solution)/shard_map/all_gather | solution.py:744
  12.7 34.8 %all-to-all-start = ((f32[128,16,128]{2,1,0:T(8,128)}), f32[128,16,128]{2,1,0:T(8,128)S(1)}, u32[]{:S(2)}, u32[]{:S(2)}) async-start(f32[128,16,128]{2,1,0:T(8,128)} %bitcast.13), calls=%async_computation | async-start | bytes 2097152 | tf_op jit(solution)/shard_map/all_to_all | solution.py:738
  48.7 1.5 copy-start
  50.1 9.3 %copy-start.1 = (f32[4,128,128]{2,1,0:T(8,128)S(1)}, f32[4,128,128]{2,1,0:T(8,128)}, u32[]{:S(2)}) copy-start(f32[4,128,128]{2,1,0:T(8,128)} %get-tuple-element.14) | copy-start | bytes 786436
  50.2 48.4 %all-to-all-start.1 = ((f32[128,40,128]{2,1,0:T(8,128)}), f32[128,40,128]{2,1,0:T(8,128)}, u32[]{:S(2)}, u32[]{:S(2)}) async-start(f32[128,40,128]{2,1,0:T(8,128)} %bitcast.11), calls=%async_computation.1 | async-start | bytes 5242880 | tf_op jit(solution)/shard_map/all_to_all | solution.py:747
  59.4 101.3 %all-gather.5.cloned.1.call-start = ((), (), s32[]{:S(2)}) async-start(), calls=%async_computation.3 | async-start | bytes 4456448 | tf_op jit(solution)/shard_map/all_gather | solution.py:749
  59.4 39.1 %collective-permute-start = (f32[512,128]{1,0:T(8,128)S(1)}, f32[512,128]{1,0:T(8,128)S(1)}, u32[]{:S(2)}, u32[]{:S(2)}) collective-permute-start(f32[512,128]{1,0:T(8,128)S(1)} %bitcast.15), channel_id=1, source_target_pairs={{0,0},{1,8},{2,16},{3,24},{4,32},{5,40},{6,48},{7,56},{8,64},{9,72... | collective-permute-start | bytes 786440 | tf_op jit(solution)/shard_map/ppermute | solution.py:743
  98.5 0.7 copy-start.2
Sparse Core Ops, SparseCore 0:
  12.8 34.7 all-gather.2
  99.4 53.6 all-gather.4
